TPU v7x, 128 devices: a whole 4x4x4 slice. The times are simulated.
128 devices in a mesh: comp: 2 (over x_hi), py: 8 (over x_lo, y), px: 8 (over z, core).
Axes of the slice: x: 4 (x_hi: 2, x_lo: 2; x = x_hi * 2 + x_lo), y: 4, z: 4, core: 2. Of those that a mesh axis runs over, the one named last changes fastest.
Arguments:
- current_speeds: float32 [2, 128, 256, 256], P(None, 'py', 'px'), may hold values from -1.2 to 1.2
- thermal_anomaly: float32 [128, 256, 256], P('py', 'px'), may hold values from -6 to 6
- solute_amounts: float32 [16, 64, 512, 256], P(None, ('py', 'px')), may hold values from -6 to 6
- delayed_link_source: float32 [2, 2, 64, 512, 256], P('comp', None, ('py', 'px')), may hold values from -6 to 6
- marine_indicator: int32 [128, 256], replicated, may hold values 0 or 1
- floor_layer_index: int32 [128, 256], replicated, may hold values from 1 to 256
- holder_rank: int32 [64, 64], replicated, may hold values from 0 to 63, each once within a row
- biota_exchange_matrix: float32 [16, 16], replicated, may hold values from -1.5 to 1.5
- photic_absorb_share: float32 [16], replicated, may hold values from -4 to 4
- chroma_loading: float32 [16], replicated, may hold values from -3 to 3
Outputs:
- coupling_out: float32 [2, 2, 64, 512, 256], P('comp', None, ('py', 'px'))
Inputs may be any that keep to these rules, and one draw needn't show every extreme that they name: `holder_rank`: each row of owner names every tracer owner once.
All inputs are finite; a program needn't handle non-finite values.
Results may differ from a plain program's by a relative error of at most 0.0001.
Values sent between devices are 32-bit elements; how exact they have to be, the bound alone decides.
A program may use at most 128 MiB of HBM per device.

v0:
```python
import jax
import jax.numpy as jnp
from jax import lax
from jax.sharding import PartitionSpec as P

NTR = 16
CY = 16
CX = 32
DEPTH_LAYERS = 256
STEPS = 3
CP = 512


advance_marine = 0.1
spreading = 0.1
viscosity = 0.1
damping = 0.05
heat_gain = 0.2
weight_pull_factor = 0.05
coriolis_scale = 1.0
step_tracer = 0.1
heating_speed = 0.06
uptake_rate = 0.01
water_absorb = (0.02, 0.003)
pigment_absorb = (0.03, 0.004)
surface_light = (40.0, 60.0)


def padded_2(array, sides, width):
    edges = {}
    for axis, dim in sides:
        peers, length = (lax.axis_size(axis), array.shape[dim])
        up = [(i, (i + 1) % peers) for i in range(peers)]
        last = lax.slice_in_dim(array, length - width, length, axis=dim)
        leading = lax.slice_in_dim(array, 0, width, axis=dim)
        edges[dim] = (
            lax.ppermute(last, axis, up),
            lax.ppermute(leading, axis, [(b, a) for a, b in up]),
        )
    done = []
    for _, dim in sides:
        low, high = edges[dim]
        around = [(width, width) if d in done else (0, 0) for d in range(array.ndim)]
        array = jnp.concatenate([jnp.pad(low, around), array, jnp.pad(high, around)], axis=dim)
        done.append(dim)
    return array


def from_partner(block, axis, stride):
    count = lax.axis_size(axis)
    route = []
    for low in range(count):
        high = low | 1 << stride
        if high != low and high < count:
            route += [(low, high), (high, low)]
    return lax.ppermute(block, axis, route)


def in_one_piece(arrays, axis, split_dim, concat_dim, along):
    both = jnp.concatenate(arrays, axis=along)
    out, at, gathered = (
        lax.all_to_all(both, axis, split_axis=split_dim, concat_axis=concat_dim, tiled=True),
        0,
        [],
    )
    for a in arrays:
        gathered.append(lax.slice_in_dim(out, at, at + a.shape[along], axis=along))
        at += a.shape[along]
    return tuple(gathered)


def in_order(blocks, dim):
    shape = list(blocks.shape[1:])
    shape[dim] *= blocks.shape[0]
    return jnp.moveaxis(blocks, 0, dim).reshape(shape)


def copy_for_each(array, axis):
    peers = lax.axis_size(axis)
    return lax.all_to_all(
        jnp.broadcast_to(array[None], (peers, *array.shape)), axis, 0, 0, tiled=True
    )


def gathered_copies(array, axis, dim):
    return in_order(copy_for_each(array, axis), dim)


def wet_levels(column_depth):
    levels = jnp.arange(DEPTH_LAYERS, dtype=jnp.int32)
    return (levels < column_depth[..., None]).astype(jnp.float32)


def layer_lookup(pattern):
    row_ids = jnp.arange(DEPTH_LAYERS, dtype=jnp.int32)[:, None]
    col_ids = jnp.arange(DEPTH_LAYERS, dtype=jnp.int32)[None, :]
    if pattern == "above":
        return jnp.where(row_ids < col_ids, 1.0, jnp.where(row_ids == col_ids, 0.5, 0.0)).astype(
            jnp.float32
        )
    if pattern == "below":
        return jnp.where(row_ids >= col_ids, 1.0, 0.0).astype(jnp.float32)
    return jnp.where(row_ids < col_ids, 1.0, 0.0).astype(jnp.float32)


def profile_product(values, table):
    return jnp.einsum("...j,jk->...k", values, table, precision=lax.Precision.HIGHEST)


def hydro_balance(thermal_grid):
    return weight_pull_factor * profile_product(thermal_grid, layer_lookup("above"))


def second_derivative_sum(values, submerged_flag):
    return (
        submerged_flag[1] * (values[1] - values[0])
        + submerged_flag[2] * (values[2] - values[0])
        + submerged_flag[3] * (values[3] - values[0])
        + submerged_flag[4] * (values[4] - values[0])
    )


def marine_interior(
    eastward_speed,
    northward_speed,
    thermal_grid,
    hydraulic_head,
    submerged_flag,
    soak_factor,
    rotation_term,
):
    eastern_boundary = (
        0.5 * (eastward_speed[0] + eastward_speed[1]) * submerged_flag[0] * submerged_flag[1]
    )
    western_boundary = (
        0.5 * (eastward_speed[2] + eastward_speed[0]) * submerged_flag[2] * submerged_flag[0]
    )
    northern_boundary = (
        0.5 * (northward_speed[0] + northward_speed[3]) * submerged_flag[0] * submerged_flag[3]
    )
    southern_boundary = (
        0.5 * (northward_speed[4] + northward_speed[0]) * submerged_flag[4] * submerged_flag[0]
    )
    carry_along = (
        eastern_boundary * 0.5 * (thermal_grid[0] + thermal_grid[1])
        - western_boundary * 0.5 * (thermal_grid[2] + thermal_grid[0])
        + northern_boundary * 0.5 * (thermal_grid[0] + thermal_grid[3])
        - southern_boundary * 0.5 * (thermal_grid[4] + thermal_grid[0])
    )
    warming_source = heat_gain * (soak_factor[0] + soak_factor[1])
    warmth_following = submerged_flag[0] * (
        thermal_grid[0]
        + advance_marine
        * (
            spreading * second_derivative_sum(thermal_grid, submerged_flag)
            - carry_along
            + warming_source
        )
    )
    zonal_push = 0.5 * (
        submerged_flag[1] * (hydraulic_head[1] - hydraulic_head[0])
        + submerged_flag[2] * (hydraulic_head[0] - hydraulic_head[2])
    )
    merid_push = 0.5 * (
        submerged_flag[3] * (hydraulic_head[3] - hydraulic_head[0])
        + submerged_flag[4] * (hydraulic_head[0] - hydraulic_head[4])
    )
    zonal_next = submerged_flag[0] * (
        eastward_speed[0]
        + advance_marine
        * (
            rotation_term * northward_speed[0]
            - zonal_push
            + viscosity * second_derivative_sum(eastward_speed, submerged_flag)
            - damping * eastward_speed[0]
        )
    )
    merid_next = submerged_flag[0] * (
        northward_speed[0]
        + advance_marine
        * (
            -rotation_term * eastward_speed[0]
            - merid_push
            + viscosity * second_derivative_sum(northward_speed, submerged_flag)
            - damping * northward_speed[0]
        )
    )
    divergence = eastern_boundary - western_boundary + northern_boundary - southern_boundary
    upright_passage = -profile_product(divergence, layer_lookup("below"))
    return (warmth_following, zonal_next, merid_next, upright_passage)


def solute_interior(
    solute_amount_status,
    upright_passage,
    thermal_grid,
    radiance_grid,
    submerged_flag,
    speed_operator,
    profit_series,
):
    empty_level = jnp.zeros_like(solute_amount_status[..., :1])
    upper_passage = jnp.concatenate(
        [
            empty_level,
            0.5
            * (solute_amount_status[..., 1:] + solute_amount_status[..., :-1])
            * upright_passage[..., 1:],
        ],
        axis=-1,
    )
    lower_passage = jnp.concatenate([upper_passage[..., 1:], empty_level], axis=-1)
    blending = jnp.einsum(
        "ij,j...->i...", speed_operator, solute_amount_status, precision=lax.Precision.HIGHEST
    )
    nutrient = solute_amount_status[0]
    saturation = nutrient * nutrient / (1.0 + nutrient * nutrient)
    expansion = uptake_rate * radiance_grid * saturation
    profit_profile = profit_series.reshape((-1,) + (1,) * (solute_amount_status.ndim - 1))
    increment = (
        jnp.exp(heating_speed * thermal_grid) * blending
        + profit_profile * expansion
        + lower_passage
        - upper_passage
    )
    return submerged_flag * (solute_amount_status + step_tracer * increment)


def light_profile(solute_amount_status, submerged_flag, weights):
    chlorophyll = jax.nn.softplus(
        jnp.einsum("f...,f->...", solute_amount_status, weights, precision=lax.Precision.HIGHEST)
    )
    prefix = layer_lookup("prefix")
    absorbed = []
    radiance_grid = jnp.zeros_like(chlorophyll)
    for band_index in range(2):
        attenuation = water_absorb[band_index] + pigment_absorb[band_index] * chlorophyll
        intensity = surface_light[band_index] * jnp.exp(-profile_product(attenuation, prefix))
        absorbed.append(submerged_flag * intensity * (1.0 - jnp.exp(-attenuation)))
        radiance_grid = radiance_grid + intensity * jnp.exp(-0.5 * attenuation)
    return (jnp.stack(absorbed), radiance_grid)


def compass(values):
    return (
        values[1:-1, 1:-1],
        values[1:-1, 2:],
        values[1:-1, :-2],
        values[2:, 1:-1],
        values[:-2, 1:-1],
    )


def marine_rim_arrays(current_speeds, thermal_anomaly):
    layer_pile = jnp.concatenate([current_speeds, thermal_anomaly[None]], axis=0)
    return padded_2(layer_pile, (("py", 1), ("px", 2)), 1)


def ocean_advance(haloed_widening, soak_factor, submerged_flag, rotation_term):
    pressure_ext = hydro_balance(haloed_widening[2])
    warmth_following, zonal_next, merid_next, upright_passage = marine_interior(
        compass(haloed_widening[0]),
        compass(haloed_widening[1]),
        compass(haloed_widening[2]),
        compass(pressure_ext),
        submerged_flag,
        soak_factor,
        rotation_term,
    )
    return (jnp.stack([zonal_next, merid_next]), warmth_following, upright_passage)


def shards(
    current_speeds,
    thermal_anomaly,
    solute_amounts,
    delayed_link_source,
    marine_indicator,
    floor_layer_index,
    holder_rank,
    biota_exchange_matrix,
    photic_absorb_share,
    chroma_loading,
):
    is_ocean = lax.axis_index("comp") == 0
    comp_index = lax.axis_index("comp")
    row_index = lax.axis_index("py")
    col_index = lax.axis_index("px")
    rows_mesh = lax.axis_size("py")
    cols_mesh = lax.axis_size("px")
    patches = rows_mesh * cols_mesh
    strip_cols = CP // patches
    patch_index = row_index * cols_mesh + col_index
    column_depth = marine_indicator * floor_layer_index
    wrapped = jnp.concatenate([column_depth[:, -1:], column_depth, column_depth[:, :1]], axis=1)
    empty_row = jnp.zeros_like(wrapped[:1])
    padded = jnp.concatenate([empty_row, wrapped, empty_row], axis=0)
    local_depth = lax.dynamic_slice(padded, (row_index * CY, col_index * CX), (CY + 2, CX + 2))
    submerged_flag = compass(wet_levels(local_depth))
    indices = jnp.arange(patches, dtype=jnp.int32)
    matches = holder_rank[:, :, None] == indices[None, None, :]
    inverse = jnp.sum(jnp.where(matches, indices[None, :, None], 0), axis=1)
    strip_of = jnp.take(inverse, patch_index, axis=1)
    in_patch = strip_of[:, None] * strip_cols + jnp.arange(strip_cols, dtype=jnp.int32)[None, :]
    glob_rows = (indices // cols_mesh)[:, None] * CY + in_patch // CX
    glob_cols = (indices % cols_mesh)[:, None] * CX + in_patch % CX
    wet_tracer = wet_levels(column_depth[glob_rows, glob_cols].reshape(CP))
    owner_row = jnp.take(holder_rank, patch_index, axis=0)
    inverse_row = jnp.take(inverse, patch_index, axis=0)
    rows_global = (row_index * CY + jnp.arange(CY, dtype=jnp.int32)).astype(jnp.float32)
    rotation_term = (coriolis_scale * (2.0 * (rows_global + 0.5) / (CY * rows_mesh) - 1.0)).reshape(
        CY, 1, 1
    )
    solute_amount_status = solute_amounts[:, 0]
    joined_fields = delayed_link_source[0, :, 0]
    half_cols = strip_cols // 2

    def own_half(values):
        blocks = values.reshape(values.shape[0], patches, strip_cols, DEPTH_LAYERS)
        return lax.dynamic_slice_in_dim(blocks, comp_index * half_cols, half_cols, 2)

    state_half = own_half(solute_amount_status).reshape(NTR, patches * half_cols, DEPTH_LAYERS)
    wet_half = own_half(wet_tracer[None])[0].reshape(patches * half_cols, DEPTH_LAYERS)
    partner_field = from_partner(joined_fields, "comp", 0)
    absorb_patch = jnp.where(is_ocean, joined_fields, partner_field)
    flux_whole = jnp.where(is_ocean, partner_field, joined_fields)
    flux_half = own_half(flux_whole).reshape(2, patches * half_cols, DEPTH_LAYERS)
    irr_half = light_profile(state_half, wet_half, chroma_loading)[1]
    for lagged in range(STEPS):
        haloed_widening = marine_rim_arrays(current_speeds, thermal_anomaly)
        current_speeds, thermal_anomaly, upright_passage = ocean_advance(
            haloed_widening,
            absorb_patch.reshape(2, CY, CX, DEPTH_LAYERS),
            submerged_flag,
            rotation_term,
        )
        state_half = solute_interior(
            state_half,
            flux_half[0],
            flux_half[1],
            irr_half,
            wet_half,
            biota_exchange_matrix,
            photic_absorb_share,
        )
        absorbed, irr_half = light_profile(state_half, wet_half, chroma_loading)
        fluxes = jnp.stack([upright_passage, thermal_anomaly]).reshape(
            2, patches, strip_cols, DEPTH_LAYERS
        )
        flux_send = lax.dynamic_slice_in_dim(
            jnp.take(fluxes, inverse_row, axis=1), comp_index * half_cols, half_cols, 2
        )
        absorb_send = absorbed.reshape(2, patches, half_cols, DEPTH_LAYERS)
        flux_back, absorb_back = in_one_piece((flux_send, absorb_send), ("py", "px"), 1, 1, 0)
        flux_half = flux_back.reshape(2, patches * half_cols, DEPTH_LAYERS)
        absorb_mine = jnp.take(absorb_back, owner_row, axis=1)
        absorb_patch = gathered_copies(absorb_mine, "comp", 2).reshape(2, CP, DEPTH_LAYERS)
    mine = flux_half.reshape(2, patches, half_cols, DEPTH_LAYERS)
    other = from_partner(mine, "comp", 0)
    joined = jnp.where(
        is_ocean, jnp.concatenate([mine, other], axis=2), jnp.concatenate([other, mine], axis=2)
    ).reshape(2, CP, DEPTH_LAYERS)
    joined_fields = jnp.where(is_ocean, absorb_patch, joined)
    return joined_fields.reshape(1, 2, 1, CP, DEPTH_LAYERS)


def solution(mesh):
    placed = (
        P(None, "py", "px", None),
        P("py", "px", None),
        P(None, ("py", "px"), None, None),
        P("comp", None, ("py", "px"), None, None),
        P(),
        P(),
        P(),
        P(),
        P(),
        P(),
    )
    return jax.shard_map(
        shards,
        mesh=mesh,
        in_specs=placed,
        out_specs=P("comp", None, ("py", "px"), None, None),
        check_vma=False,
    )
```

profile of v0, /device:TPU:2, one launch (start us, length us, event | category | flops | bytes accessed | tf_op | source)
XLA Modules:
  0.0 292.8 jit_solution(6794867021113475208)
XLA Ops:
  3.1 2.6 collective-permute-start.2
  7.6 3.0 %collective-permute-start.3 = (f32[3,16,1,256]{3,2,1,0:T(1,128)}, f32[3,16,1,256]{3,2,1,0:T(1,128)}, u32[]{:S(2)}, u32[]{:S(2)}) collective-permute-start(f32[3,16,1,256]{3,2,1,0:T(1,128)} %get-tuple-element.71), channel_id=1, source_target_pairs={{1,0},{2,1},{3,2},{4,3},{5,4},{6,5},{7,6},{0,7},{9,8},{10,9},{11,1... | collective-permute-start | bytes 147464 | tf_op jit(solution)/shard_map/ppermute | solution.py:38
  16.6 4.7 %gather_fusion = s32[512]{0:T(512)S(1)} fusion(s32[128,256]{1,0:T(8,128)S(1)} %mul.799, s32[512]{0:T(512)S(1)} %reshape.544), kind=kCustom, calls=%fused_computation.6 | custom fusion | bytes 8192 | tf_op jit(solution)/shard_map/gather | solution.py:307
  21.7 4.3 %constant_dynamic-slice_fusion.3 = f32[16,64,4,256]{3,2,1,0:T(4,128)S(1)} fusion(f32[16,64,8,256]{3,2,1,0:T(8,128)} %bitcast.313, s32[]{:T(128)S(6)} %select_n.222), kind=kLoop, calls=%fused_computation.421 | loop fusion | bytes 8388612 | tf_op jit(solution)/shard_map/dynamic_slice | solution.py:320
  26.0 2.4 copy.114
  34.3 2.4 fusion.47
  42.6 2.4 add_multiply_fusion.2
  48.3 6.7 %fusion.2 = f32[16,256,255]{2,0,1:T(8,128)} fusion(f32[16,256,256]{2,0,1:T(8,128)} %bitcast.297, f32[256,255]{1,0:T(8,128)S(1)} %slice_multiply_fusion.5), kind=kLoop, calls=%fused_computation.12 | loop fusion | flops 2088960 | bytes 12794880 | tf_op jit(solution)/shard_map/mul | solution.py:206
  57.9 11.8 %fusion.17 = f32[16,256,256]{2,0,1:T(8,128)S(1)} fusion(f32[16,256,256]{2,0,1:T(8,128)} %bitcast.298, f32[16,256,255]{2,0,1:T(8,128)} %fusion.2, f32[256,256]{1,0:T(8,128)} %fusion.47, f32[16]{0:T(128)S(1)} %copy-done.19, f32[256,256]{1,0:T(8,128)S(1)} %exp.104, f32[256,256]{1,0:T(8,128)S(1)} %reshape_squeeze.6, f32[16,16]{1,0:T(8,128)S(1)} %copy-done), kind=kOutput, calls=%fused_computation.30 | convolution fusion | flops 209715200 | bytes 13354048 | tf_op jit(solution)/shard_map/ij,j...->i.../dot_general | solution.py:213
  69.8 2.3 fusion.262
  73.1 4.6 %collective-permute-start.7 = (f32[3,1,32,256]{3,2,1,0:T(8,128)S(1)}, f32[3,1,32,256]{3,2,1,0:T(8,128)}, u32[]{:S(2)}, u32[]{:S(2)}) collective-permute-start(f32[3,1,32,256]{3,2,1,0:T(8,128)S(1)} %get-tuple-element.65), channel_id=1, source_target_pairs={{8,0},{16,8},{24,16},{32,24},{40,32},{48,40},{56,48},{0,56},{9,1},... | collective-permute-start | bytes 294920 | tf_op jit(solution)/shard_map/ppermute | solution.py:38
  77.7 3.0 %collective-permute-start.8 = (f32[3,16,1,256]{3,2,1,0:T(1,128)}, f32[3,16,1,256]{3,2,1,0:T(1,128)}, u32[]{:S(2)}, u32[]{:S(2)}) collective-permute-start(f32[3,16,1,256]{3,2,1,0:T(1,128)} %get-tuple-element.67), channel_id=1, source_target_pairs={{1,0},{2,1},{3,2},{4,3},{5,4},{6,5},{7,6},{0,7},{9,8},{10,9},{11,1... | collective-permute-start | bytes 147464 | tf_op jit(solution)/shard_map/ppermute | solution.py:38
  82.3 2.8 gather_fusion.1
  87.1 2.7 fusion.151
  94.7 6.5 %all-to-all-start = ((f32[4,64,4,256]{3,2,0,1:T(4,128)}), f32[4,64,4,256]{3,2,0,1:T(4,128)}, u32[]{:S(2)}, u32[]{:S(2)}) async-start(f32[4,64,4,256]{3,2,0,1:T(4,128)} %pad_maximum_fusion.1), calls=%async_computation | async-start | bytes 2097152 | tf_op jit(solution)/shard_map/all_to_all | solution.py:62
  106.5 12.2 %all-to-all-done = f32[4,64,4,256]{3,2,0,1:T(4,128)} async-done(((f32[4,64,4,256]{3,2,0,1:T(4,128)}), f32[4,64,4,256]{3,2,0,1:T(4,128)}, u32[]{:S(2)}, u32[]{:S(2)}) %all-to-all-start) | async-done | bytes 1048608 | tf_op jit(solution)/shard_map/all_to_all | solution.py:62
  120.6 2.7 gather_fusion.2
  125.7 4.6 %all-to-all-start.1 = ((f32[2,2,64,4,256]{4,3,2,1,0:T(4,128)}), f32[2,2,64,4,256]{4,3,2,1,0:T(4,128)}, u32[]{:S(2)}, u32[]{:S(2)}) async-start(f32[2,2,64,4,256]{4,3,2,1,0:T(4,128)} %broadcast_in_dim.160), calls=%async_computation.1 | async-start | bytes 2097152 | tf_op jit(solution)/shard_map/all_to_all | solution.py:80
  133.4 6.7 %fusion.1 = f32[16,256,255]{2,0,1:T(8,128)} fusion(f32[16,256,256]{2,0,1:T(8,128)} %copy-done.2, f32[256,255]{1,0:T(8,128)S(1)} %slice_multiply_fusion.3), kind=kLoop, calls=%fused_computation.10 | loop fusion | flops 2088960 | bytes 12794880 | tf_op jit(solution)/shard_map/mul | solution.py:206
  141.2 11.8 %fusion.12 = f32[16,256,256]{2,0,1:T(8,128)S(1)} fusion(f32[16,256,256]{2,0,1:T(8,128)} %copy-done.2, f32[16,256,255]{2,0,1:T(8,128)} %fusion.1, f32[256,256]{1,0:T(8,128)} %get-tuple-element.81, f32[256,256]{1,0:T(8,128)S(1)} %exp.116, f32[16]{0:T(128)S(1)} %copy-done.19, f32[256,256]{1,0:T(8,128)S(1)} %reshape_squeeze.6, f32[16,16]{1,0:T(8,128)S(1)} %copy-done), kind=kOutput, calls=%fused_computation.24 | convolution fusion | flops 209715200 | bytes 13354048 | tf_op jit(solution)/shard_map/ij,j...->i.../dot_general | solution.py:213
  168.8 5.4 %all-to-all-start.2 = ((f32[4,64,4,256]{3,2,0,1:T(4,128)}), f32[4,64,4,256]{3,2,0,1:T(4,128)}, u32[]{:S(2)}, u32[]{:S(2)}) async-start(f32[4,64,4,256]{3,2,0,1:T(4,128)} %pad_maximum_fusion.3), calls=%async_computation.2 | async-start | bytes 2097152 | tf_op jit(solution)/shard_map/all_to_all | solution.py:62
  175.8 2.6 collective-permute-start.11
  180.3 7.9 %fusion.251 = f32[256,256,16]{1,2,0:T(8,128)} fusion(f32[16,256,256]{2,0,1:T(8,128)} %copy-done.1, f32[16,16]{1,0:T(8,128)S(1)} %copy-done), kind=kOutput, calls=%fused_computation.410 | convolution fusion | flops 201326592 | bytes 8389632 | tf_op jit(solution)/shard_map/ij,j...->i.../dot_general | solution.py:213
  188.2 2.5 collective-permute-done.10
  197.4 5.0 %all-to-all-start.3 = ((f32[2,2,64,4,256]{4,3,2,1,0:T(4,128)}), f32[2,2,64,4,256]{4,3,2,1,0:T(4,128)}, u32[]{:S(2)}, u32[]{:S(2)}) async-start(f32[2,2,64,4,256]{4,3,2,1,0:T(4,128)} %broadcast_in_dim.162), calls=%async_computation.3 | async-start | bytes 2097152 | tf_op jit(solution)/shard_map/all_to_all | solution.py:80
  204.6 6.8 %fusion = f32[16,256,255]{2,0,1:T(8,128)} fusion(f32[16,256,256]{2,0,1:T(8,128)} %copy-done.1, f32[256,255]{1,0:T(8,128)S(1)} %slice_multiply_fusion), kind=kLoop, calls=%fused_computation.8 | loop fusion | flops 2088960 | bytes 12794880 | tf_op jit(solution)/shard_map/mul | solution.py:206
  212.4 9.8 %fusion.18 = f32[1,256,256]{2,0,1:T(1,128)S(1)} fusion(f32[16,256,256]{2,0,1:T(8,128)} %copy-done.1, f32[16,256,255]{2,0,1:T(8,128)} %fusion, f32[256,256,16]{1,2,0:T(8,128)} %fusion.251, f32[256,256]{1,0:T(8,128)} %get-tuple-element.78, f32[256,256]{1,0:T(8,128)S(1)} %exp.125, f32[16]{0:T(128)S(1)} %copy-done.19, f32[256,256]{1,0:T(8,128)S(1)} %copy-done.9, ...), kind=kOutput, calls=%fused_computation.31 | convolution fusion | flops 20971520 | bytes 13615232 | tf_op jit(solution)/shard_map/f...,f->.../dot_general | solution.py:231
  233.2 23.7 %all_to_all.30 = f32[4,64,4,256]{3,2,0,1:T(4,128)S(1)} all-to-all(f32[4,64,4,256]{3,2,0,1:T(4,128)S(1)} %pad_maximum_fusion.5), channel_id=1, replica_groups=mesh['comp'=2,'py'=8,'px'=8] {'py','px'}, dimensions={1} | all-to-all | bytes 2097152 | tf_op jit(solution)/shard_map/all_to_all | solution.py:62
  259.3 4.8 %all-to-all-start.5 = ((f32[2,2,64,4,256]{4,3,2,1,0:T(4,128)}), f32[2,2,64,4,256]{4,3,2,1,0:T(4,128)S(1)}, u32[]{:S(2)}, u32[]{:S(2)}) async-start(f32[2,2,64,4,256]{4,3,2,1,0:T(4,128)} %broadcast_in_dim.163), calls=%async_computation.5 | async-start | bytes 2097152 | tf_op jit(solution)/shard_map/all_to_all | solution.py:80
  264.1 3.8 %collective-permute-start.13 = (f32[2,64,4,256]{3,2,0,1:T(4,128)S(1)}, f32[2,64,4,256]{3,2,0,1:T(4,128)S(1)}, u32[]{:S(2)}, u32[]{:S(2)}) collective-permute-start(f32[2,64,4,256]{3,2,0,1:T(4,128)S(1)} %get-tuple-element.73), channel_id=1, source_target_pairs={{0,64},{64,0},{1,65},{65,1},{2,66},{66,2},{3,67},{67,3},{4,68},{68... | collective-permute-start | bytes 1572872 | tf_op jit(solution)/shard_map/ppermute | solution.py:56
  267.9 12.7 %all-to-all-done.5 = f32[2,2,64,4,256]{4,3,2,1,0:T(4,128)S(1)} async-done(((f32[2,2,64,4,256]{4,3,2,1,0:T(4,128)}), f32[2,2,64,4,256]{4,3,2,1,0:T(4,128)S(1)}, u32[]{:S(2)}, u32[]{:S(2)}) %all-to-all-start.5) | async-done | bytes 1048608 | tf_op jit(solution)/shard_map/all_to_all | solution.py:80
  281.4 8.3 %collective-permute-done.13 = f32[2,64,4,256]{3,2,0,1:T(4,128)S(1)} collective-permute-done((f32[2,64,4,256]{3,2,0,1:T(4,128)S(1)}, f32[2,64,4,256]{3,2,0,1:T(4,128)S(1)}, u32[]{:S(2)}, u32[]{:S(2)}) %collective-permute-start.13) | collective-permute-done | bytes 524320 | tf_op jit(solution)/shard_map/ppermute | solution.py:56
  (186 shorter events, 97.8 us)
Async XLA Ops:
  0.0 57.9 %copy-start = (f32[16,16]{1,0:T(8,128)S(1)}, f32[16,16]{1,0:T(8,128)}, u32[]{:S(2)}) copy-start(f32[16,16]{1,0:T(8,128)} %param.23) | copy-start | bytes 3076
  1.6 35.3 %collective-permute-start.1 = (f32[3,1,32,256]{3,2,1,0:T(8,128)}, f32[3,1,32,256]{3,2,1,0:T(8,128)}, u32[]{:S(2)}, u32[]{:S(2)}) collective-permute-start(f32[3,1,32,256]{3,2,1,0:T(8,128)} %get-tuple-element.68), channel_id=1, source_target_pairs={{0,8},{8,16},{16,24},{24,32},{32,40},{40,48},{48,56},{56,0},{1,9},... | collective-permute-start | bytes 294920 | tf_op jit(solution)/shard_map/ppermute | solution.py:37
  3.1 33.7 %collective-permute-start.2 = (f32[3,1,32,256]{3,2,1,0:T(8,128)S(1)}, f32[3,1,32,256]{3,2,1,0:T(8,128)}, u32[]{:S(2)}, u32[]{:S(2)}) collective-permute-start(f32[3,1,32,256]{3,2,1,0:T(8,128)S(1)} %get-tuple-element.69), channel_id=1, source_target_pairs={{8,0},{16,8},{24,16},{32,24},{40,32},{48,40},{56,48},{0,56},{9,1},... | collective-permute-start | bytes 294920 | tf_op jit(solution)/shard_map/ppermute | solution.py:38
  7.6 29.2 %collective-permute-start = (f32[3,16,1,256]{3,2,1,0:T(1,128)}, f32[3,16,1,256]{3,2,1,0:T(1,128)S(1)}, u32[]{:S(2)}, u32[]{:S(2)}) collective-permute-start(f32[3,16,1,256]{3,2,1,0:T(1,128)} %get-tuple-element.70), channel_id=1, source_target_pairs={{0,1},{1,2},{2,3},{3,4},{4,5},{5,6},{6,7},{7,0},{8,9},{9,10},{10,1... | collective-permute-start | bytes 147464 | tf_op jit(solution)/shard_map/ppermute | solution.py:37
  7.6 29.2 %collective-permute-start.3 = (f32[3,16,1,256]{3,2,1,0:T(1,128)}, f32[3,16,1,256]{3,2,1,0:T(1,128)}, u32[]{:S(2)}, u32[]{:S(2)}) collective-permute-start(f32[3,16,1,256]{3,2,1,0:T(1,128)} %get-tuple-element.71), channel_id=1, source_target_pairs={{1,0},{2,1},{3,2},{4,3},{5,4},{6,5},{7,6},{0,7},{9,8},{10,9},{11,1... | collective-permute-start | bytes 147464 | tf_op jit(solution)/shard_map/ppermute | solution.py:38
  10.5 30.0 %collective-permute-start.4 = (f32[2,512,256]{2,1,0:T(8,128)}, f32[2,512,256]{2,1,0:T(8,128)}, u32[]{:S(2)}, u32[]{:S(2)}) collective-permute-start(f32[2,512,256]{2,1,0:T(8,128)} %bitcast.318), channel_id=1, source_target_pairs={{0,64},{64,0},{1,65},{65,1},{2,66},{66,2},{3,67},{67,3},{4,68},{68... | collective-permute-start | bytes 3145736 | tf_op jit(solution)/shard_map/ppermute | solution.py:56
  26.0 4.4 %copy-start.18 = (f32[16]{0:T(128)S(1)}, f32[16]{0:T(128)}, u32[]{:S(2)}) copy-start(f32[16]{0:T(128)} %param.25) | copy-start | bytes 196
  32.7 4.1 %copy-start.4 = (f32[2,16,32,256]{3,2,1,0:T(8,128)S(1)}, f32[2,16,32,256]{3,2,1,0:T(8,128)}, u32[]{:S(2)}) copy-start(f32[2,16,32,256]{3,2,1,0:T(8,128)} %param.16) | copy-start | bytes 3145732
  32.8 4.1 %copy-start.7 = (f32[16,32,256]{2,1,0:T(8,128)S(1)}, f32[16,32,256]{2,1,0:T(8,128)}, u32[]{:S(2)}) copy-start(f32[16,32,256]{2,1,0:T(8,128)} %param.17) | copy-start | bytes 1572868
  36.8 119.3 %copy-start.8 = (f32[256,256]{1,0:T(8,128)}, f32[256,256]{1,0:T(8,128)S(1)}, u32[]{:S(2)}) copy-start(f32[256,256]{1,0:T(8,128)S(1)} %reshape_squeeze.6) | copy-start | bytes 786436
  48.3 9.6 %copy-start.19 = (f32[16]{0:T(128)S(1)}, f32[16]{0:T(128)}, u32[]{:S(2)}) copy-start(f32[16]{0:T(128)} %param.24) | copy-start | bytes 196
  69.8 10.9 %copy-start.11 = (f32[16,32,256]{2,1,0:T(8,128)S(1)}, f32[16,32,256]{2,1,0:T(8,128)}, u32[]{:S(2)}) copy-start(f32[16,32,256]{2,1,0:T(8,128)} %get-tuple-element.46) | copy-start | bytes 1572868
  69.8 10.9 %copy-start.12 = (f32[16,32,256]{2,1,0:T(8,128)S(1)}, f32[16,32,256]{2,1,0:T(8,128)}, u32[]{:S(2)}) copy-start(f32[16,32,256]{2,1,0:T(8,128)} %get-tuple-element.47) | copy-start | bytes 1572868
  69.8 10.8 %copy-start.13 = (f32[16,32,256]{2,1,0:T(8,128)S(1)}, f32[16,32,256]{2,1,0:T(8,128)}, u32[]{:S(2)}) copy-start(f32[16,32,256]{2,1,0:T(8,128)} %get-tuple-element.48) | copy-start | bytes 1572868
  73.1 28.2 %collective-permute-start.6 = (f32[3,1,32,256]{3,2,1,0:T(8,128)}, f32[3,1,32,256]{3,2,1,0:T(8,128)}, u32[]{:S(2)}, u32[]{:S(2)}) collective-permute-start(f32[3,1,32,256]{3,2,1,0:T(8,128)} %get-tuple-element.64), channel_id=1, source_target_pairs={{0,8},{8,16},{16,24},{24,32},{32,40},{40,48},{48,56},{56,0},{1,9},... | collective-permute-start | bytes 294920 | tf_op jit(solution)/shard_map/ppermute | solution.py:37
  73.1 28.2 %collective-permute-start.7 = (f32[3,1,32,256]{3,2,1,0:T(8,128)S(1)}, f32[3,1,32,256]{3,2,1,0:T(8,128)}, u32[]{:S(2)}, u32[]{:S(2)}) collective-permute-start(f32[3,1,32,256]{3,2,1,0:T(8,128)S(1)} %get-tuple-element.65), channel_id=1, source_target_pairs={{8,0},{16,8},{24,16},{32,24},{40,32},{48,40},{56,48},{0,56},{9,1},... | collective-permute-start | bytes 294920 | tf_op jit(solution)/shard_map/ppermute | solution.py:38
  77.7 23.6 %collective-permute-start.5 = (f32[3,16,1,256]{3,2,1,0:T(1,128)}, f32[3,16,1,256]{3,2,1,0:T(1,128)S(1)}, u32[]{:S(2)}, u32[]{:S(2)}) collective-permute-start(f32[3,16,1,256]{3,2,1,0:T(1,128)} %get-tuple-element.66), channel_id=1, source_target_pairs={{0,1},{1,2},{2,3},{3,4},{4,5},{5,6},{6,7},{7,0},{8,9},{9,10},{10,1... | collective-permute-start | bytes 147464 | tf_op jit(solution)/shard_map/ppermute | solution.py:37
  77.7 23.6 %collective-permute-start.8 = (f32[3,16,1,256]{3,2,1,0:T(1,128)}, f32[3,16,1,256]{3,2,1,0:T(1,128)}, u32[]{:S(2)}, u32[]{:S(2)}) collective-permute-start(f32[3,16,1,256]{3,2,1,0:T(1,128)} %get-tuple-element.67), channel_id=1, source_target_pairs={{1,0},{2,1},{3,2},{4,3},{5,4},{6,5},{7,6},{0,7},{9,8},{10,9},{11,1... | collective-permute-start | bytes 147464 | tf_op jit(solution)/shard_map/ppermute | solution.py:38
  94.7 24.0 %all-to-all-start = ((f32[4,64,4,256]{3,2,0,1:T(4,128)}), f32[4,64,4,256]{3,2,0,1:T(4,128)}, u32[]{:S(2)}, u32[]{:S(2)}) async-start(f32[4,64,4,256]{3,2,0,1:T(4,128)} %pad_maximum_fusion.1), calls=%async_computation | async-start | bytes 2097152 | tf_op jit(solution)/shard_map/all_to_all | solution.py:62
  125.7 34.6 %all-to-all-start.1 = ((f32[2,2,64,4,256]{4,3,2,1,0:T(4,128)}), f32[2,2,64,4,256]{4,3,2,1,0:T(4,128)}, u32[]{:S(2)}, u32[]{:S(2)}) async-start(f32[2,2,64,4,256]{4,3,2,1,0:T(4,128)} %broadcast_in_dim.160), calls=%async_computation.1 | async-start | bytes 2097152 | tf_op jit(solution)/shard_map/all_to_all | solution.py:80
  153.0 4.8 %copy-start.1 = (f32[16,256,256]{2,0,1:T(8,128)}, f32[16,256,256]{2,0,1:T(8,128)S(1)}, u32[]{:S(2)}) copy-start(f32[16,256,256]{2,0,1:T(8,128)S(1)} %fusion.12) | copy-start | bytes 12582916
  166.2 8.0 %copy-start.5 = (f32[1,16,32,256]{3,2,1,0:T(8,128)S(1)}, f32[1,16,32,256]{3,2,1,0:T(8,128)}, u32[]{:S(2)}) copy-start(f32[1,16,32,256]{3,2,1,0:T(8,128)} %fusion.98) | copy-start | bytes 1572868
  166.2 8.0 %copy-start.6 = (f32[1,16,32,256]{3,2,1,0:T(8,128)S(1)}, f32[1,16,32,256]{3,2,1,0:T(8,128)}, u32[]{:S(2)}) copy-start(f32[1,16,32,256]{3,2,1,0:T(8,128)} %fusion.83) | copy-start | bytes 1572868
  168.8 23.6 %all-to-all-start.2 = ((f32[4,64,4,256]{3,2,0,1:T(4,128)}), f32[4,64,4,256]{3,2,0,1:T(4,128)}, u32[]{:S(2)}, u32[]{:S(2)}) async-start(f32[4,64,4,256]{3,2,0,1:T(4,128)} %pad_maximum_fusion.3), calls=%async_computation.2 | async-start | bytes 2097152 | tf_op jit(solution)/shard_map/all_to_all | solution.py:62
  174.3 16.5 %collective-permute-start.10 = (f32[3,1,32,256]{3,2,1,0:T(8,128)S(1)}, f32[3,1,32,256]{3,2,1,0:T(8,128)S(1)}, u32[]{:S(2)}, u32[]{:S(2)}) collective-permute-start(f32[3,1,32,256]{3,2,1,0:T(8,128)S(1)} %get-tuple-element.60), channel_id=1, source_target_pairs={{0,8},{8,16},{16,24},{24,32},{32,40},{40,48},{48,56},{56,0},{1,9},... | collective-permute-start | bytes 294920 | tf_op jit(solution)/shard_map/ppermute | solution.py:37
  175.8 14.9 %collective-permute-start.11 = (f32[3,1,32,256]{3,2,1,0:T(8,128)S(1)}, f32[3,1,32,256]{3,2,1,0:T(8,128)S(1)}, u32[]{:S(2)}, u32[]{:S(2)}) collective-permute-start(f32[3,1,32,256]{3,2,1,0:T(8,128)S(1)} %get-tuple-element.61), channel_id=1, source_target_pairs={{8,0},{16,8},{24,16},{32,24},{40,32},{48,40},{56,48},{0,56},{9,1},... | collective-permute-start | bytes 294920 | tf_op jit(solution)/shard_map/ppermute | solution.py:38
  178.5 9.8 %collective-permute-start.12 = (f32[3,16,1,256]{3,2,1,0:T(1,128)S(1)}, f32[3,16,1,256]{3,2,1,0:T(1,128)S(1)}, u32[]{:S(2)}, u32[]{:S(2)}) collective-permute-start(f32[3,16,1,256]{3,2,1,0:T(1,128)S(1)} %get-tuple-element.63), channel_id=1, source_target_pairs={{1,0},{2,1},{3,2},{4,3},{5,4},{6,5},{7,6},{0,7},{9,8},{10,9},{11,1... | collective-permute-start | bytes 147464 | tf_op jit(solution)/shard_map/ppermute | solution.py:38
  180.3 7.9 %collective-permute-start.9 = (f32[3,16,1,256]{3,2,1,0:T(1,128)S(1)}, f32[3,16,1,256]{3,2,1,0:T(1,128)S(1)}, u32[]{:S(2)}, u32[]{:S(2)}) collective-permute-start(f32[3,16,1,256]{3,2,1,0:T(1,128)S(1)} %get-tuple-element.62), channel_id=1, source_target_pairs={{0,1},{1,2},{2,3},{3,4},{4,5},{5,6},{6,7},{7,0},{8,9},{9,10},{10,1... | collective-permute-start | bytes 147464 | tf_op jit(solution)/shard_map/ppermute | solution.py:37
  197.4 29.5 %all-to-all-start.3 = ((f32[2,2,64,4,256]{4,3,2,1,0:T(4,128)}), f32[2,2,64,4,256]{4,3,2,1,0:T(4,128)}, u32[]{:S(2)}, u32[]{:S(2)}) async-start(f32[2,2,64,4,256]{4,3,2,1,0:T(4,128)} %broadcast_in_dim.162), calls=%async_computation.3 | async-start | bytes 2097152 | tf_op jit(solution)/shard_map/all_to_all | solution.py:80
  204.6 7.9 %copy-start.9 = (f32[256,256]{1,0:T(8,128)S(1)}, f32[256,256]{1,0:T(8,128)}, u32[]{:S(2)}) copy-start(f32[256,256]{1,0:T(8,128)} %copy-done.8) | copy-start | bytes 786436
  259.3 21.3 %all-to-all-start.5 = ((f32[2,2,64,4,256]{4,3,2,1,0:T(4,128)}), f32[2,2,64,4,256]{4,3,2,1,0:T(4,128)S(1)}, u32[]{:S(2)}, u32[]{:S(2)}) async-start(f32[2,2,64,4,256]{4,3,2,1,0:T(4,128)} %broadcast_in_dim.163), calls=%async_computation.5 | async-start | bytes 2097152 | tf_op jit(solution)/shard_map/all_to_all | solution.py:80
  264.1 25.7 %collective-permute-start.13 = (f32[2,64,4,256]{3,2,0,1:T(4,128)S(1)}, f32[2,64,4,256]{3,2,0,1:T(4,128)S(1)}, u32[]{:S(2)}, u32[]{:S(2)}) collective-permute-start(f32[2,64,4,256]{3,2,0,1:T(4,128)S(1)} %get-tuple-element.73), channel_id=1, source_target_pairs={{0,64},{64,0},{1,65},{65,1},{2,66},{66,2},{3,67},{67,3},{4,68},{68... | collective-permute-start | bytes 1572872 | tf_op jit(solution)/shard_map/ppermute | solution.py:56
  (11 other events, 21.6 us)
where the time goes:
time: 299 us; the launch traced here: 293 us
  other arithmetic  64.7 us (22%)
  matrix products  63 us (21%)
  starting transfers between devices  52.9 us (18%)
  local copies, waits for them, and re-layouts  50.1 us (17%)
  waiting for transfers between devices  36.9 us (12%)
  blocking collectives  23.7 us (8%)
    dot_general x3, matrix products, solute_interior(): jnp.einsum('ij,j...->i...', speed_operator, solute_amount_status, precisi...  31.5 us
    all_to_all x1, blocking collectives, in_one_piece(): lax.all_to_all(both, axis, split_axis=split_dim, concat_axis=concat_dim,...  23.7 us
    mul x6, other arithmetic, solute_interior(): 0.5 * (solute_amount_status[..., 1:] + solute_amount_status[..., :-1])  21.5 us
    ppermute x6, starting transfers between devices, padded_2(): lax.ppermute(leading, axis, [(b, a) for a, b in up])  17.5 us
    dot_general x4, matrix products, light_profile(): jnp.einsum('f...,f->...', solute_amount_status, weights, precision=lax.Pr...  16.8 us
    dot_general x13, matrix products, profile_product(): jnp.einsum('...j,jk->...k', values, table, precision=lax.Precision.HIGHEST)  14.7 us
    all_to_all x3, starting transfers between devices, copy_for_each(): lax.all_to_all(jnp.broadcast_to(array[None], (peers, *array.shape)), axis...  14.4 us
    all_to_all x2, waiting for transfers between devices, in_one_piece(): lax.all_to_all(both, axis, split_axis=split_dim, concat_axis=concat_dim,...  13.3 us
  transfers between devices with their start and end apart: 19, of which 5 were waited for; matrix products, arithmetic and copies ran while one was open for 37% of the time, Pallas kernels for 0%

commit v1 on v0

v1 whole, which is shorter than its diff:
```python
import jax
import jax.numpy as jnp
from jax import lax
from jax.experimental import pallas as pl
from jax.experimental.pallas import tpu as pltpu
from jax.sharding import PartitionSpec as P

NTR = 16
CY = 16
CX = 32
K = 256
NP = 64
SC = 8
NS = 32
F32 = jnp.float32
BF16 = jnp.bfloat16
MESH = pl.DeviceIdType.MESH


def split(x):
    hi = x.astype(BF16)
    lo = (x - hi.astype(F32)).astype(BF16)
    return hi, lo


def dot(a, b):
    return jnp.dot(a, b, preferred_element_type=F32)


def dot_two(x, table):
    hi, lo = split(x)
    return dot(hi, table) + dot(lo, table)


def kernel(
    inv_s,
    own_s,
    share_s,
    load_s,
    speeds,
    thermal,
    solute,
    link,
    depth_o,
    depth_t,
    mix,
    out,
    b0,
    b1,
    b2,
    press,
    wet_o,
    tabs,
    wmix,
    conc,
    chl_b,
    irr,
    tfl,
    div,
    rise,
    bands0,
    asum0,
    f0r,
    f1s,
    f1r,
    f2s,
    f2r,
    f3s,
    f3r,
    own1,
    own2,
    a1r,
    a2r,
    a3s,
    a3r,
    dummy,
    edge_s,
    edge_r,
    lsem,
    hs_sem,
    hr_sem,
    xs_sem,
    xr_sem,
):
    c = lax.axis_index("comp")
    py = lax.axis_index("py")
    px = lax.axis_index("px")
    me = py * 8 + px
    par = lax.rem(c + me, 2)
    half = lax.div(me, 2)

    def dev(cc, rr):
        return (cc, lax.div(rr, 8), lax.rem(rr, 8))

    ld_uv = pltpu.make_async_copy(speeds, b0.at[0:2, 1:17, 8:40, :], lsem.at[0])
    ld_t = pltpu.make_async_copy(thermal, b0.at[2, 1:17, 8:40, :], lsem.at[1])
    ld_c = pltpu.make_async_copy(solute.at[:, :, par], conc, lsem.at[2])
    ld_uv.start()
    ld_t.start()

    @pl.when(c == 0)
    def _():
        pltpu.make_async_copy(link, bands0, lsem.at[3]).start()

    @pl.when(c == 1)
    def _():
        for f in range(2):
            pltpu.make_async_copy(link.at[f, :, par], f0r.at[:, f], lsem.at[4 + f]).start()

    ld_c.start()

    barrier = pltpu.get_barrier_semaphore()
    flat = c * 64 + me

    @pl.loop(1, 128)
    def _(i):
        d = lax.rem(flat + i, 128)
        pl.semaphore_signal(
            barrier,
            inc=1,
            device_id=(lax.div(d, 64), lax.rem(lax.div(d, 8), 8), lax.rem(d, 8)),
            device_id_type=MESH,
        )

    rows = lax.broadcasted_iota(jnp.int32, (K, K), 0)
    cols = lax.broadcasted_iota(jnp.int32, (K, K), 1)
    tabs[0] = jnp.where(rows < cols, 1.0, jnp.where(rows == cols, 0.5, 0.0)).astype(BF16)
    tabs[1] = jnp.where(rows >= cols, 1.0, 0.0).astype(BF16)
    tabs[2] = jnp.where(rows < cols, 1.0, 0.0).astype(BF16)
    r16 = lax.broadcasted_iota(jnp.int32, (128, 16), 0)
    c16 = lax.broadcasted_iota(jnp.int32, (128, 16), 1)
    spread = jnp.where(lax.shift_right_logical(r16, 3) == c16, 1.0, 0.0).astype(F32)
    r16t = lax.broadcasted_iota(jnp.int32, (16, 128), 0)
    c16t = lax.broadcasted_iota(jnp.int32, (16, 128), 1)
    spread_t = jnp.where(lax.shift_right_logical(c16t, 3) == r16t, 1.0, 0.0).astype(F32)
    wide = jnp.dot(
        jnp.dot(spread, mix[...], precision=lax.Precision.HIGHEST, preferred_element_type=F32),
        spread_t,
        precision=lax.Precision.HIGHEST,
        preferred_element_type=F32,
    )
    r128 = lax.broadcasted_iota(jnp.int32, (128, 128), 0)
    c128 = lax.broadcasted_iota(jnp.int32, (128, 128), 1)
    same = lax.bitwise_and(r128, 7) == lax.bitwise_and(c128, 7)
    wide = jnp.where(same, wide, 0.0)
    whi, wlo = split(wide)
    wmix[0:128, 0:128] = whi
    wmix[0:128, 128:256] = whi
    wmix[128:256, 0:128] = wlo
    wmix[128:256, 128:256] = jnp.zeros((128, 128), BF16)

    lev48 = lax.broadcasted_iota(jnp.int32, (48, 128), 1)

    @pl.loop(0, 18)
    def _(y):
        d = depth_o[y]
        wet_o[y, :, 0:128] = jnp.where(lev48 < d, 1.0, 0.0).astype(F32)
        wet_o[y, :, 128:256] = jnp.where(lev48 + 128 < d, 1.0, 0.0).astype(F32)

    north = (c, lax.rem(py + 1, 8), px)
    south = (c, lax.rem(py + 7, 8), px)
    east = (c, py, lax.rem(px + 1, 8))
    west = (c, py, lax.rem(px + 7, 8))

    def edge_copies(e, b):
        def rc(src, dst, j, who):
            return pltpu.make_async_remote_copy(
                src_ref=src,
                dst_ref=dst,
                send_sem=hs_sem.at[e, j],
                recv_sem=hr_sem.at[e, j],
                device_id=who,
                device_id_type=MESH,
            )

        return (
            rc(b.at[:, 16, 8:40, :], b.at[:, 0, 8:40, :], 0, north),
            rc(b.at[:, 1, 8:40, :], b.at[:, 17, 8:40, :], 1, south),
            rc(edge_s.at[e, 0], edge_r.at[e, 0], 2, east),
            rc(edge_s.at[e, 1], edge_r.at[e, 1], 3, west),
        )

    def stage_edges(e, b):
        for f in range(3):
            edge_s[e, 0, f] = b[f, 1:17, pl.ds(39, 1), :].reshape(CY, K)
            edge_s[e, 1, f] = b[f, 1:17, pl.ds(8, 1), :].reshape(CY, K)

    def send_edges(e, b):
        for copy in edge_copies(e, b):
            copy.start()

    def take_edges(e, b):
        for copy in edge_copies(e, b):
            copy.wait_recv()
        for f in range(3):
            b[f, 1:17, pl.ds(7, 1), :] = edge_r[e, 0, f].reshape(CY, 1, K)
            b[f, 1:17, pl.ds(40, 1), :] = edge_r[e, 1, f].reshape(CY, 1, K)

    def wait_edge_sends(e, b):
        for copy in edge_copies(e, b):
            copy.wait_send()

    def ocean(b, bo, with_flow):
        if with_flow:

            @pl.loop(0, 18)
            def _(y):
                press[y] = 0.05 * dot_two(b[2, y], tabs[0])

        @pl.loop(0, CY)
        def _(y):
            yy = y + 1
            line = (py * CY + y).astype(F32)
            rot = 2.0 * (line + 0.5) / 128.0 - 1.0
            for xb in range(4):
                x0 = 8 + 8 * xb

                def five(ref):
                    return (
                        ref[yy, pl.ds(x0, 8), :],
                        ref[yy, pl.ds(x0 + 1, 8), :],
                        ref[yy, pl.ds(x0 - 1, 8), :],
                        ref[yy + 1, pl.ds(x0, 8), :],
                        ref[yy - 1, pl.ds(x0, 8), :],
                    )

                w = five(wet_o)
                u = five(b.at[0])
                v = five(b.at[1])
                t = five(b.at[2])

                def lap(x):
                    return (
                        w[1] * (x[1] - x[0])
                        + w[2] * (x[2] - x[0])
                        + w[3] * (x[3] - x[0])
                        + w[4] * (x[4] - x[0])
                    )

                wh = 0.5 * w[0]
                fe = (u[0] + u[1]) * (wh * w[1])
                fw = (u[2] + u[0]) * (wh * w[2])
                fn = (v[0] + v[3]) * (wh * w[3])
                fs = (v[4] + v[0]) * (wh * w[4])
                adv = 0.5 * (
                    fe * (t[0] + t[1])
                    - fw * (t[2] + t[0])
                    + fn * (t[0] + t[3])
                    - fs * (t[4] + t[0])
                )
                tn = w[0] * (t[0] + 0.1 * (0.1 * lap(t) - adv))
                s = y * 4 + xb
                tfl[s] = tn
                div[s] = fe - fw + fn - fs
                if with_flow:
                    p = five(press)
                    gx = 0.5 * (w[1] * (p[1] - p[0]) + w[2] * (p[0] - p[2]))
                    gy = 0.5 * (w[3] * (p[3] - p[0]) + w[4] * (p[0] - p[4]))
                    un = w[0] * (
                        u[0] + 0.1 * (rot * v[0] - gx + 0.1 * lap(u) - 0.05 * u[0])
                    )
                    vn = w[0] * (
                        v[0] + 0.1 * (-rot * u[0] - gy + 0.1 * lap(v) - 0.05 * v[0])
                    )
                    bo[0, yy, pl.ds(x0, 8), :] = un
                    bo[1, yy, pl.ds(x0, 8), :] = vn
                    bo[2, yy, pl.ds(x0, 8), :] = tn

        @pl.loop(0, 4)
        def _(i):
            d = div[pl.ds(i * 16, 16)].reshape(128, K)
            rise[pl.ds(i * 16, 16)] = -dot_two(d, tabs[1]).reshape(16, 8, K)

    lev8 = lax.broadcasted_iota(jnp.int32, (8, 128), 1)
    lane = lax.broadcasted_iota(jnp.int32, (8, K), 1)

    def wet_of(n):
        d = depth_t[n]
        return jnp.concatenate(
            [
                jnp.where(lev8 < d, 1.0, 0.0).astype(F32),
                jnp.where(lev8 + 128 < d, 1.0, 0.0).astype(F32),
            ],
            axis=1,
        )

    def first_chl():
        @pl.loop(0, NS)
        def _(n):
            total = load_s[0] * conc[0, n]
            for i in range(1, NTR):
                total = total + load_s[i] * conc[i, n]
            chl_b[n] = total

    def tracer(flux, extra):
        @pl.loop(0, NS)
        def _(n):
            up = flux[n, 0]
            heat = flux[n, 1]
            if extra is not None:
                heat = heat + 0.02 * extra[n]
            wet = wet_of(n)
            warm = (0.1 * wet) * jnp.exp(0.06 * heat)
            scaled = (0.05 * wet) * up
            lower = jnp.where(lane == 0, 0.0, scaled)
            upper = jnp.where(lane == K - 1, 0.0, (0.05 * wet) * pltpu.roll(up, K - 1, 1))
            stay = wet + upper - lower
            c0 = conc[0, n]
            sq = c0 * c0
            grow = (0.001 * wet) * irr[n] * (sq / (1.0 + sq))
            x = conc[:, n].reshape(128, K)
            hi, lo = split(x)
            y = dot(wmix[...], jnp.concatenate([hi, lo], axis=0))
            total = None
            for i in range(NTR):
                ci = conc[i, n]
                blend = y[8 * i : 8 * i + 8] + y[128 + 8 * i : 136 + 8 * i]
                new = (
                    stay * ci
                    + warm * blend
                    + upper * pltpu.roll(ci, K - 1, 1)
                    - lower * pltpu.roll(ci, 1, 1)
                    + share_s[i] * grow
                )
                conc[i, n] = new
                part = load_s[i] * new
                total = part if total is None else total + part
            chl_b[n] = total

    lev_f = lax.broadcasted_iota(jnp.int32, (64, K), 1).astype(F32)

    def light(dest):
        @pl.loop(0, 4)
        def _(i):
            sl = pl.ds(i * 8, 8)
            x = chl_b[sl].reshape(64, K)
            chl = jnp.maximum(x, 0.0) + jnp.log1p(jnp.exp(-jnp.abs(x)))
            pre = dot_two(chl, tabs[2])
            i0 = 40.0 * jnp.exp(-(0.02 * lev_f + 0.03 * pre))
            i1 = 60.0 * jnp.exp(-(0.003 * lev_f + 0.004 * pre))
            h0 = jnp.exp(-0.5 * (0.02 + 0.03 * chl))
            h1 = jnp.exp(-0.5 * (0.003 + 0.004 * chl))
            if dest is not a3s:
                irr[sl] = (i0 * h0 + i1 * h1).reshape(8, 8, K)
            if dest is not None:
                wet = jnp.concatenate([wet_of(i * 8 + j) for j in range(8)], axis=0)
                m0 = wet * i0 * (1.0 - h0 * h0)
                m1 = wet * i1 * (1.0 - h1 * h1)
                if dest is a3s:
                    dest[sl, 0] = m0.reshape(8, 8, K)
                    dest[sl, 1] = m1.reshape(8, 8, K)
                else:
                    dest[sl] = (m0 + m1).reshape(8, 8, K)

    def remote(src, dst, x, who):
        return pltpu.make_async_remote_copy(
            src_ref=src,
            dst_ref=dst,
            send_sem=xs_sem.at[x],
            recv_sem=xr_sem.at[x],
            device_id=who,
            device_id_type=MESH,
        )

    def drain(ref, sem):
        pltpu.make_async_copy(ref, ref, sem).wait()

    def local_twice(src, dst, x):
        pltpu.make_async_copy(src, dst, xr_sem.at[x]).start()
        pltpu.make_async_copy(src, dummy.at[x], xs_sem.at[x]).start()

    def send_flux(x, fs, fr):
        @pl.loop(0, NS)
        def _(m):
            s = inv_s[2 * m + par]
            fs[m, 0] = rise[s]
            fs[m, 1] = tfl[s]

        @pl.loop(0, NS)
        def _(i):
            m = lax.rem(half + i, NS)
            r = 2 * m + par

            @pl.when(r != me)
            def _():
                remote(fs.at[m], fr.at[half], x, dev(c, r)).start()

            @pl.when(r == me)
            def _():
                local_twice(fs.at[m], fr.at[half], x)

    ld_uv.wait()
    ld_t.wait()
    stage_edges(0, b0)
    pl.semaphore_wait(barrier, 127)
    send_edges(0, b0)

    @pl.when(c == 0)
    def _():
        pltpu.make_async_copy(link, bands0, lsem.at[3]).wait()

        @pl.loop(0, 8)
        def _(i):
            sl = pl.ds(i * 4, 4)
            asum0[sl] = bands0[0, sl] + bands0[1, sl]

        remote(asum0, asum0, 0, (1, py, px)).start()

    @pl.when(c == 1)
    def _():
        for f in range(2):
            remote(link.at[f, :, 1 - par], f0r.at[:, f], 1 + f, (0, py, px)).start()
        for f in range(2):
            pltpu.make_async_copy(link.at[f, :, par], f0r.at[:, f], lsem.at[4 + f]).wait()

    ld_c.wait()
    first_chl()
    light(None)
    take_edges(0, b0)
    ocean(b0, b1, True)

    @pl.when(c == 1)
    def _():
        remote(asum0, asum0, 0, (1, py, px)).wait_recv()

    @pl.loop(0, CY)
    def _(y):
        for xb in range(4):
            sl = (y + 1, pl.ds(8 + 8 * xb, 8))
            s = y * 4 + xb
            two = lax.div(s, 2)
            new = tfl[s] + 0.02 * wet_o[y + 1, pl.ds(8 + 8 * xb, 8), :] * asum0[two, xb % 2]
            tfl[s] = new
            b1[2, y + 1, pl.ds(8 + 8 * xb, 8), :] = new

    stage_edges(1, b1)
    send_edges(1, b1)
    send_flux(3, f1s, f1r)

    @pl.when(c == 0)
    def _():
        for f in range(2):
            remote(link.at[f, :, 1 - par], f0r.at[:, f], 1 + f, (0, py, px)).wait_recv()

    tracer(f0r, None)
    light(own1)

    @pl.loop(0, NS)
    def _(i):
        n = lax.rem(half + i, NS)
        remote(own1.at[n], a1r.at[me], 5, dev(1, 2 * n + par)).start()

    take_edges(1, b1)
    ocean(b1, b2, True)
    send_flux(4, f2s, f2r)

    drain(f1r, xr_sem.at[3])
    tracer(f1r, None)
    light(own2)

    @pl.when(c == 0)
    def _():
        remote(own2, a2r, 6, (1, py, px)).start()

    @pl.when(c == 1)
    def _():
        drain(a1r, xr_sem.at[5])

        @pl.loop(0, CY)
        def _(y):
            for xb in range(4):
                s = y * 4 + xb
                b2[2, y + 1, pl.ds(8 + 8 * xb, 8), :] = tfl[s] + 0.02 * a1r[own_s[s]]

        stage_edges(2, b2)
        send_edges(2, b2)
        take_edges(2, b2)
        ocean(b2, None, False)

        @pl.loop(0, NP)
        def _(r):
            s = inv_s[r]
            f3s[r, 0] = rise[s]
            f3s[r, 1] = tfl[s]

        @pl.loop(0, NP)
        def _(i):
            r = lax.rem(me + i, NP)

            @pl.when(r != me)
            def _():
                remote(f3s.at[r], f3r.at[me], 7, dev(1, r)).start()

            @pl.when(r == me)
            def _():
                local_twice(f3s.at[r], f3r.at[me], 7)

    drain(f2r, xr_sem.at[4])
    tracer(f2r, own1)
    light(a3s)

    @pl.loop(0, NS)
    def _(i):
        n = lax.rem(half + i, NS)
        q = 2 * n + par

        @pl.when((c == 1) | (q != me))
        def _():
            remote(a3s.at[n], a3r.at[me], 8, dev(0, q)).start()

        @pl.when((c == 0) & (q == me))
        def _():
            local_twice(a3s.at[n], a3r.at[me], 8)

    wait_edge_sends(0, b0)
    wait_edge_sends(1, b1)
    drain(f1s, xs_sem.at[3])
    drain(f2s, xs_sem.at[4])
    drain(own1, xs_sem.at[5])

    @pl.when(c == 0)
    def _():
        remote(asum0, asum0, 0, (1, py, px)).wait_send()
        remote(own2, a2r, 6, (1, py, px)).wait_send()
        drain(a3r, xr_sem.at[8])

        @pl.loop(0, NP)
        def _(s):
            r = own_s[s]
            out[0, s] = a3r[r, 0]
            out[1, s] = a3r[r, 1]

    @pl.when(c == 1)
    def _():
        for f in range(2):
            remote(link.at[f, :, 1 - par], f0r.at[:, f], 1 + f, (0, py, px)).wait_send()
        wait_edge_sends(2, b2)
        drain(f3s, xs_sem.at[7])
        remote(own2, a2r, 6, (1, py, px)).wait_recv()
        drain(f3r, xr_sem.at[7])

        @pl.loop(0, NS)
        def _(n):
            mine = 2 * n + par
            other = 2 * n + (1 - par)
            out[0, mine] = f3r[mine, 0]
            out[0, other] = f3r[other, 0]
            out[1, mine] = f3r[mine, 1] + 0.02 * own2[n]
            out[1, other] = f3r[other, 1] + 0.02 * a2r[n]

    drain(a3s, xs_sem.at[8])


def shards(
    current_speeds,
    thermal_anomaly,
    solute_amounts,
    delayed_link_source,
    marine_indicator,
    floor_layer_index,
    holder_rank,
    biota_exchange_matrix,
    photic_absorb_share,
    chroma_loading,
):
    comp = lax.axis_index("comp")
    py = lax.axis_index("py")
    px = lax.axis_index("px")
    me = py * 8 + px
    par = (comp + me) % 2
    depth = marine_indicator * floor_layer_index
    wrapped = jnp.concatenate([depth[:, -8:], depth, depth[:, :8]], axis=1)
    padded = jnp.pad(wrapped, ((1, 1), (0, 0)))
    local = lax.dynamic_slice(padded, (py * CY, px * CX), (CY + 2, CX + 16))
    depth_o = jnp.broadcast_to(local[:, :, None], (CY + 2, CX + 16, 128))
    own_row = lax.dynamic_index_in_dim(holder_rank, me, 0, keepdims=False)
    ids = jnp.arange(NP, dtype=jnp.int32)
    inv_row = jnp.sum(jnp.where(own_row[:, None] == ids[None, :], ids[:, None], 0), axis=0)
    hit = (holder_rank == me).reshape(8, 8, 16, 4)
    blocks = depth.reshape(8, 16, 8, 4, 8)
    strip = jnp.sum(jnp.where(hit.transpose(0, 2, 1, 3)[..., None], blocks, 0), axis=(1, 3))
    mine = lax.dynamic_index_in_dim(strip.reshape(NS, 2, SC), par, 1, keepdims=False)
    depth_t = jnp.broadcast_to(mine[:, :, None], (NS, SC, 128))

    any_spec = pl.BlockSpec(memory_space=pl.ANY)
    vmem = pl.BlockSpec(memory_space=pltpu.VMEM)
    smem = pl.BlockSpec(memory_space=pltpu.SMEM)

    def v(*shape, dtype=F32):
        return pltpu.VMEM(shape, dtype)

    dma = pltpu.SemaphoreType.DMA
    res = pl.pallas_call(
        kernel,
        out_shape=jax.ShapeDtypeStruct((2, NP, SC, K), F32),
        in_specs=[smem] * 4 + [any_spec] * 4 + [vmem] * 3,
        out_specs=vmem,
        scratch_shapes=[
            v(3, 18, 48, K),
            v(3, 18, 48, K),
            v(3, 18, 48, K),
            v(18, 48, K),
            v(18, 48, K),
            v(3, K, K, dtype=BF16),
            v(K, K, dtype=BF16),
            v(NTR, NS, SC, K),
            v(NS, SC, K),
            v(NS, SC, K),
            v(NP, SC, K),
            v(NP, SC, K),
            v(NP, SC, K),
            v(2, NS, 2, SC, K),
            v(NS, 2, SC, K),
            v(NS, 2, SC, K),
            v(NS, 2, SC, K),
            v(NS, 2, SC, K),
            v(NS, 2, SC, K),
            v(NS, 2, SC, K),
            v(NP, 2, SC, K),
            v(NP, 2, SC, K),
            v(NS, SC, K),
            v(NS, SC, K),
            v(NP, SC, K),
            v(NS, SC, K),
            v(NS, 2, SC, K),
            v(NP, 2, SC, K),
            v(9, 2, SC, K),
            v(3, 2, 3, CY, K),
            v(3, 2, 3, CY, K),
            dma((6,)),
            dma((3, 4)),
            dma((3, 4)),
            dma((9,)),
            dma((9,)),
        ],
        compiler_params=pltpu.CompilerParams(
            collective_id=0, has_side_effects=True, vmem_limit_bytes=60 * 1024 * 1024
        ),
    )(
        inv_row.astype(jnp.int32),
        own_row,
        photic_absorb_share,
        chroma_loading,
        current_speeds,
        thermal_anomaly,
        solute_amounts.reshape(NTR, NS, 2, SC, K),
        delayed_link_source.reshape(2, NS, 2, SC, K),
        depth_o,
        depth_t,
        biota_exchange_matrix,
    )
    return res.reshape(1, 2, 1, 512, K)


def solution(mesh):
    placed = (
        P(None, "py", "px", None),
        P("py", "px", None),
        P(None, ("py", "px"), None, None),
        P("comp", None, ("py", "px"), None, None),
        P(),
        P(),
        P(),
        P(),
        P(),
        P(),
    )
    return jax.shard_map(
        shards,
        mesh=mesh,
        in_specs=placed,
        out_specs=P("comp", None, ("py", "px"), None, None),
        check_vma=False,
    )
```

time: 299 us -> 94.6 us (0.32)
  the two profiles are of different devices: /device:TPU:2 before, /device:TPU:25 now
where the time goes in v1:
time: 94.6 us; the launch traced here: 94.3 us
  Pallas kernels  84.7 us (90%)
  local copies, waits for them, and re-layouts  5.83 us (6%)
  other arithmetic  3.72 us (4%)
    pallas_call x1, Pallas kernels, shards(): pl.pallas_call(kernel, out_shape=jax.ShapeDtypeStruct((2, NP, SC, K), F32...  84.7 us
    unnamed x3, local copies, waits for them, and re-layouts  2.27 us

profile of v1, /device:TPU:25, one launch (start us, length us, event | category | flops | bytes accessed | tf_op | source)
XLA Modules:
  0.0 94.3 jit_solution(9875307454140361040)
XLA Ops:
  0.0 0.7 dynamic-slice_bitcast_fusion.own_s
  0.7 0.0 copy-start
  0.7 0.7 select_reduce_fusion.1.inv_s
  1.4 0.8 broadcast_compare_fusion
  2.1 0.1 copy.22
  2.2 0.2 reshape.26
  2.4 0.3 copy.23
  2.7 1.0 %mul.13 = s32[128,256]{1,0:T(8,128)S(1)} multiply(s32[128,256]{1,0:T(8,128)} %param.14, s32[128,256]{1,0:T(8,128)} %param.15) | non-fusion elementwise | flops 32768 | bytes 393216 | tf_op jit(solution)/shard_map/mul | solution.py:571
  3.6 0.1 copy.24
  3.7 0.1 fusion
  3.8 0.1 pad_add_fusion
  4.0 0.1 pad_dynamic-slice_fusion
  4.1 0.9 broadcast_in_dim.44.depth_o
  5.0 0.3 reshape.27
  5.3 1.2 %select_reduce_fusion = s32[8,8,8]{0,2,1:T(8,128)S(1)} fusion(s32[8,16,8,4,8]{1,0,4,3,2:T(8,128)S(1)} %reshape.27, pred[8,16,8,4]{1,0,3,2:T(8,128)(4,1)S(1)} %copy.23), kind=kLoop, calls=%fused_computation | loop fusion | flops 65024 | bytes 137216 | tf_op jit(solution)/shard_map/reduce_sum | solution.py:581
  6.5 0.1 copy.25
  6.6 0.7 broadcast_in_dim.48.depth_t
  7.4 0.0 copy-done
  7.4 84.7 %shard_map.100 = f32[2,64,8,256]{3,2,1,0:T(8,128)} custom-call(s32[64]{0:T(128)} %select_reduce_fusion.1.inv_s, s32[64]{0:T(128)} %copy-done, f32[16]{0:T(128)} %share_s.1, f32[16]{0:T(128)} %load_s.1, f32[2,16,32,256]{3,2,1,0:T(8,128)} %speeds.1, f32[16,32,256]{2,1,0:T(8,128)} %thermal.1, f32[16,32,2,8,256]{4,3,2,1,0:T(8,128)} %bitcast.14, ...), custom_call_target="tpu_custom_call" | custom-call | tf_op jit(solution)/shard_map/pallas_call | solution.py:593
  92.0 2.3 %copy.28 = f32[1,2,1,512,256]{4,3,2,1,0:T(8,128)} copy(f32[1,2,1,512,256]{4,3,2,1,0:T(8,128)} %bitcast.15) | data formatting | bytes 2097152
  (1 shorter events, 0.0 us)
Async XLA Ops:
  0.7 6.7 %copy-start = (s32[64]{0:T(128)}, s32[64]{0:T(128)S(1)}, u32[]{:S(2)}) copy-start(s32[64]{0:T(128)S(1)} %dynamic-slice_bitcast_fusion.own_s) | copy-start | bytes 772

commit v2 on v1

v2 whole, which is shorter than its diff:
```python
import jax
import jax.numpy as jnp
from jax import lax
from jax.experimental import pallas as pl
from jax.experimental.pallas import tpu as pltpu
from jax.sharding import PartitionSpec as P

NTR = 16
CY = 16
CX = 32
K = 256
NP = 64
SC = 8
NS = 32
F32 = jnp.float32
BF16 = jnp.bfloat16
MESH = pl.DeviceIdType.MESH


def split(x):
    hi = x.astype(BF16)
    lo = (x - hi.astype(F32)).astype(BF16)
    return hi, lo


def dot(a, b):
    return jnp.dot(a, b, preferred_element_type=F32)


def dot_two(x, table):
    hi, lo = split(x)
    return dot(hi, table) + dot(lo, table)


def kernel(
    own_s,
    share_s,
    load_s,
    speeds,
    thermal,
    solute,
    link,
    marine,
    floor,
    owners,
    mix,
    out,
    inv_v,
    inv_s,
    depth,
    depth_t,
    pick,
    face_x,
    face_y,
    south_f,
    mixed_a,
    mixed_b,
    b0,
    b1,
    b2,
    press,
    wet_o,
    tabs,
    wmix,
    conc,
    chl_b,
    irr,
    tfl,
    div,
    rise,
    bands0,
    asum0,
    f0r,
    f1s,
    f1r,
    f2s,
    f2r,
    f3s,
    f3r,
    own1,
    own2,
    a1r,
    a2r,
    a3r,
    dummy,
    edge_s,
    edge_r,
    lsem,
    hs_sem,
    hr_sem,
    xs_sem,
    xr_sem,
):
    c = lax.axis_index("comp")
    py = lax.axis_index("py")
    px = lax.axis_index("px")
    me = py * 8 + px
    par = lax.rem(c + me, 2)
    half = lax.div(me, 2)

    def dev(cc, rr):
        return (cc, lax.div(rr, 8), lax.rem(rr, 8))

    def spot_of(i):
        return jnp.minimum(jnp.maximum(inv_s[0, i], 0), NP - 1)

    ld_uv = pltpu.make_async_copy(speeds, b0.at[0:2, 1:17, 0:32, :], lsem.at[0])
    ld_t = pltpu.make_async_copy(thermal, b0.at[2, 1:17, 0:32, :], lsem.at[1])
    ld_c = pltpu.make_async_copy(solute.at[:, :, par], conc, lsem.at[2])

    def ld_link(f):
        return pltpu.make_async_copy(link.at[f, :, par], f0r.at[:, f], lsem.at[4 + f])

    ld_uv.start()
    ld_t.start()

    @pl.when(c == 0)
    def _():
        pltpu.make_async_copy(link, bands0, lsem.at[3]).start()

    @pl.when(c == 1)
    def _():
        for f in range(2):
            ld_link(f).start()

    ld_c.start()

    barrier = pltpu.get_barrier_semaphore()
    for dc in range(2):
        for db in range(8):

            @pl.loop(1 if dc == 0 and db == 0 else 0, 8)
            def _(a, dc=dc, db=db):
                pl.semaphore_signal(
                    barrier,
                    inc=1,
                    device_id=(lax.rem(c + dc, 2), lax.rem(py + a, 8), lax.rem(px + db, 8)),
                    device_id_type=MESH,
                )

    step64 = lax.broadcasted_iota(jnp.int32, (NP, NP), 1).astype(F32)
    row64 = lax.broadcasted_iota(jnp.int32, (NP, NP), 0)
    held = jnp.where(owners[...] == me, 1.0, 0.0).astype(F32)
    placed = jnp.where(
        jnp.broadcast_to(owners[pl.ds(me, 1), :], (NP, NP)) == row64, 1.0, 0.0
    ).astype(F32)
    nt = (((1,), (1,)), ((), ()))
    steps8 = step64[0:8]
    for j, spots in enumerate((placed, held)):
        found = lax.dot_general(steps8, spots, nt, preferred_element_type=F32)
        inv_v[0:8, 64 * j : 64 * j + 64] = jnp.minimum(found, NP - 1.0).astype(jnp.int32)
    to_smem = pltpu.make_async_copy(inv_v, inv_s, lsem.at[6])
    to_smem.start()

    rows = lax.broadcasted_iota(jnp.int32, (K, K), 0)
    cols = lax.broadcasted_iota(jnp.int32, (K, K), 1)
    tabs[0] = jnp.where(rows < cols, 1.0, jnp.where(rows == cols, 0.5, 0.0)).astype(BF16)
    tabs[1] = jnp.where(rows >= cols, 1.0, 0.0).astype(BF16)
    tabs[2] = jnp.where(rows < cols, 1.0, 0.0).astype(BF16)
    r16 = lax.broadcasted_iota(jnp.int32, (128, 16), 0)
    c16 = lax.broadcasted_iota(jnp.int32, (128, 16), 1)
    spread = jnp.where(lax.shift_right_logical(r16, 3) == c16, 1.0, 0.0).astype(F32)
    r16t = lax.broadcasted_iota(jnp.int32, (16, 128), 0)
    c16t = lax.broadcasted_iota(jnp.int32, (16, 128), 1)
    spread_t = jnp.where(lax.shift_right_logical(c16t, 3) == r16t, 1.0, 0.0).astype(F32)
    wide = jnp.dot(
        jnp.dot(spread, mix[...], precision=lax.Precision.HIGHEST, preferred_element_type=F32),
        spread_t,
        precision=lax.Precision.HIGHEST,
        preferred_element_type=F32,
    )
    r128 = lax.broadcasted_iota(jnp.int32, (128, 128), 0)
    c128 = lax.broadcasted_iota(jnp.int32, (128, 128), 1)
    same = lax.bitwise_and(r128, 7) == lax.bitwise_and(c128, 7)
    wide = jnp.where(same, wide, 0.0)
    whi, wlo = split(wide)
    wmix[0:128, 0:128] = whi
    wmix[0:128, 128:256] = whi
    wmix[128:256, 0:128] = wlo
    wmix[128:256, 128:256] = jnp.zeros((128, 128), BF16)

    ones = jnp.ones((K, 128), BF16)
    depth[...] = (marine[...] * floor[...]).astype(F32)
    lev40 = lax.broadcasted_iota(jnp.int32, (40, 128), 1).astype(F32)
    spot = lax.broadcasted_iota(jnp.int32, (40, K), 0)
    spot = jnp.where(spot < 36, spot, spot - 40)
    column = lax.broadcasted_iota(jnp.int32, (40, K), 1)
    chosen = lax.bitwise_and(spot + (px * CX + K), K - 1) == column

    @pl.loop(0, 18)
    def _(y):
        gy = py * CY + y - 1
        inside = jnp.logical_and(gy >= 0, gy < 128)
        line = depth[pl.ds(jnp.clip(gy, 0, 127), 1), :]
        line = line * jnp.where(inside, 1.0, 0.0).astype(F32)
        d = dot(jnp.where(chosen, line, 0.0).astype(BF16), ones)
        w = jnp.concatenate(
            [
                jnp.where(lev40 < d, 1.0, 0.0).astype(F32),
                jnp.where(lev40 + 128.0 < d, 1.0, 0.0).astype(F32),
            ],
            axis=1,
        )
        wet_o[y] = w
        face_x[y] = w * pltpu.roll(w, 39, 0)

    @pl.loop(0, 17)
    def _(y):
        face_y[y] = wet_o[y, 0:32, :] * wet_o[y + 1, 0:32, :]

    to_smem.wait()
    ahead = lax.broadcasted_iota(jnp.int32, (8, K), 1) - lax.broadcasted_iota(
        jnp.int32, (8, K), 0
    )

    @pl.loop(0, NS)
    def _(n):
        q = 2 * n + par
        s = spot_of(64 + q)
        line = depth[lax.div(q, 8) * CY + lax.shift_right_logical(s, 2)]
        x0 = lax.rem(q, 8) * CX + lax.bitwise_and(s, 3) * 8
        pick[n] = jnp.where(ahead == x0, jnp.broadcast_to(line[None, :], (8, K)), 0.0)

    depth_t[...] = dot(pick[...].reshape(NS * 8, K).astype(BF16), ones).reshape(NS, 8, 128)

    north = (c, lax.rem(py + 1, 8), px)
    south = (c, lax.rem(py + 7, 8), px)
    east = (c, py, lax.rem(px + 1, 8))
    west = (c, py, lax.rem(px + 7, 8))

    def edge_copies(e, b, lo, hi):
        def rc(src, dst, j, who):
            return pltpu.make_async_remote_copy(
                src_ref=src,
                dst_ref=dst,
                send_sem=hs_sem.at[e, j],
                recv_sem=hr_sem.at[e, j],
                device_id=who,
                device_id_type=MESH,
            )

        return (
            rc(b.at[lo:hi, 16, 0:32, :], b.at[lo:hi, 0, 0:32, :], 0, north),
            rc(b.at[lo:hi, 1, 0:32, :], b.at[lo:hi, 17, 0:32, :], 1, south),
            rc(edge_s.at[e, 0, lo:hi], edge_r.at[e, 0, lo:hi], 2, east),
            rc(edge_s.at[e, 1, lo:hi], edge_r.at[e, 1, lo:hi], 3, west),
        )

    def send_edges(e, b, lo=0, hi=3):
        for f in range(lo, hi):
            edge_s[e, 0, f] = b[f, 1:17, pl.ds(31, 1), :].reshape(CY, K)
            edge_s[e, 1, f] = b[f, 1:17, pl.ds(0, 1), :].reshape(CY, K)
        if e == 0:
            pl.semaphore_wait(barrier, 127)
        for copy in edge_copies(e, b, lo, hi):
            copy.start()

    def take_edges(e, b, lo=0, hi=3):
        for copy in edge_copies(e, b, lo, hi):
            copy.wait_recv()
        for f in range(lo, hi):
            b[f, 1:17, pl.ds(39, 1), :] = edge_r[e, 0, f].reshape(CY, 1, K)
            b[f, 1:17, pl.ds(32, 1), :] = edge_r[e, 1, f].reshape(CY, 1, K)

    def wait_edge_sends(e, b, lo=0, hi=3):
        for copy in edge_copies(e, b, lo, hi):
            copy.wait_send()

    def ocean(b, bo, flow, heat, passage):
        if flow:

            @pl.loop(0, 6)
            def _(i):
                sl = pl.ds(i * 3, 3)
                t = b[2, sl].reshape(120, K)
                press[sl] = dot_two(t, tabs[0]).reshape(3, 40, K)

        def faces(m, a, t, tn, n, o, on, p, pn):
            through = (0.5 * m) * (a + n)
            m1 = 0.01 * m
            g = first = second = side = None
            if heat:
                g = m1 * (tn - t) - (0.05 * through) * (t + tn)
            if flow:
                spread_a = m1 * (n - a)
                push = (0.05 * 0.05 * m) * (pn - p)
                first = spread_a - push
                second = spread_a + push
                side = m1 * (on - o)
            return through, g, first, second, side

        def face_north(y):
            def pair(ref):
                return ref[y, 0:32, :], ref[y + 1, 0:32, :]

            v, vn = pair(b.at[1])
            t, tn = pair(b.at[2]) if heat else (None, None)
            u, un = pair(b.at[0]) if flow else (None, None)
            p, pn = pair(press) if flow else (None, None)
            return faces(face_y[y], v, t, tn, vn, u, un, p, pn)

        def keep(values):
            for i, value in enumerate(values):
                if value is not None:
                    south_f[i] = value

        keep(face_north(0))

        @pl.loop(0, CY)
        def _(y):
            yy = y + 1

            def pair(ref):
                x = ref[yy]
                return x, pltpu.roll(x, 39, 0)

            def west_of(x):
                return pltpu.roll(x, 1, 0)[0:32]

            u, ue = pair(b.at[0])
            t, te = pair(b.at[2]) if heat else (None, None)
            v, ve = pair(b.at[1]) if flow else (None, None)
            p, pe = pair(press) if flow else (None, None)
            f, g, first, second, side = faces(face_x[yy], u, t, te, ue, v, ve, p, pe)
            north_f = face_north(yy)
            fn, gn, first_n, second_n, side_n = north_f
            s4 = pl.ds(y * 4, 4)
            if passage:
                d = f[0:32] - west_of(f) + fn - south_f[0]
                div[s4] = d.reshape(4, 8, K)
            if heat or flow:
                w = wet_o[yy, 0:32, :]
            if heat:
                new = w * t[0:32] + (g[0:32] - west_of(g)) + (gn - south_f[1])
                tfl[s4] = new.reshape(4, 8, K)
            if flow:
                line = (py * CY + y).astype(F32)
                turn = 0.1 * (2.0 * (line + 0.5) / 128.0 - 1.0)
                wu = w * u[0:32]
                wv = w * v[0:32]
                bo[0, yy, 0:32, :] = (
                    (0.995 * wu + turn * wv)
                    + (first[0:32] - west_of(second))
                    + (side_n - south_f[4])
                )
                bo[1, yy, 0:32, :] = (
                    (0.995 * wv - turn * wu)
                    + (side[0:32] - west_of(side))
                    + (first_n - south_f[3])
                )
            keep(north_f)

        if passage:

            @pl.loop(0, 4)
            def _(i):
                d = div[pl.ds(i * 16, 16)].reshape(128, K)
                rise[pl.ds(i * 16, 16)] = -dot_two(d, tabs[1]).reshape(16, 8, K)

    lev8 = lax.broadcasted_iota(jnp.int32, (8, 128), 1).astype(F32)
    lane = lax.broadcasted_iota(jnp.int32, (8, K), 1)

    def wet_of(n):
        d = depth_t[n]
        return jnp.concatenate(
            [
                jnp.where(lev8 < d, 1.0, 0.0).astype(F32),
                jnp.where(lev8 + 128.0 < d, 1.0, 0.0).astype(F32),
            ],
            axis=1,
        )

    def first_chl():
        @pl.loop(0, NS)
        def _(n):
            total = load_s[0] * conc[0, n]
            for i in range(1, NTR):
                total = total + load_s[i] * conc[i, n]
            chl_b[n] = total

    def mingle(n, dest):
        hi_x, lo_x = split(conc[:, n].reshape(128, K))
        y = dot(wmix[...], jnp.concatenate([hi_x, lo_x], axis=0))
        dest[...] = y[0:128] + y[128:256]

    def tracer(flux, extra, lo, hi):
        def advance(n, mixed):
            up = flux[n, 0]
            heat = flux[n, 1]
            if extra is not None:
                heat = heat + 0.02 * extra[n]
            wet = wet_of(n)
            warm = (0.1 * wet) * jnp.exp(0.06 * heat)
            scaled = (0.05 * wet) * up
            lower = jnp.where(lane == 0, 0.0, scaled)
            upper = jnp.where(lane == K - 1, 0.0, (0.05 * wet) * pltpu.roll(up, K - 1, 1))
            stay = wet + upper - lower
            c0 = conc[0, n]
            sq = c0 * c0
            grow = (0.001 * wet) * irr[n] * (sq / (1.0 + sq))
            total = None
            for i in range(NTR):
                ci = conc[i, n]
                new = (
                    stay * ci
                    + warm * mixed[8 * i : 8 * i + 8]
                    + upper * pltpu.roll(ci, K - 1, 1)
                    - lower * pltpu.roll(ci, 1, 1)
                    + share_s[i] * grow
                )
                conc[i, n] = new
                part = load_s[i] * new
                total = part if total is None else total + part
            chl_b[n] = total

        mingle(lo, mixed_a)

        @pl.loop(0, (hi - lo) // 2)
        def _(k):
            n = lo + 2 * k
            mingle(n + 1, mixed_b)
            advance(n, mixed_a)
            mingle(jnp.minimum(n + 2, hi - 1), mixed_a)
            advance(n + 1, mixed_b)

    lev_f = lax.broadcasted_iota(jnp.int32, (64, K), 1).astype(F32)

    def bands_of(x):
        chl = jnp.maximum(x, 0.0) + jnp.log1p(jnp.exp(-jnp.abs(x)))
        pre = dot_two(chl, tabs[2])
        i0 = 40.0 * jnp.exp(-(0.02 * lev_f + 0.03 * pre))
        i1 = 60.0 * jnp.exp(-(0.003 * lev_f + 0.004 * pre))
        h0 = jnp.exp(-0.5 * (0.02 + 0.03 * chl))
        h1 = jnp.exp(-0.5 * (0.003 + 0.004 * chl))
        return i0, i1, h0, h1

    def light(dest):
        @pl.loop(0, 4)
        def _(i):
            sl = pl.ds(i * 8, 8)
            i0, i1, h0, h1 = bands_of(chl_b[sl].reshape(64, K))
            irr[sl] = (i0 * h0 + i1 * h1).reshape(8, 8, K)
            if dest is not None:
                wet = jnp.concatenate([wet_of(i * 8 + j) for j in range(8)], axis=0)
                total = wet * (i0 * (1.0 - h0 * h0) + i1 * (1.0 - h1 * h1))
                dest[sl] = total.reshape(8, 8, K)

    def remote(src, dst, x, who):
        return pltpu.make_async_remote_copy(
            src_ref=src,
            dst_ref=dst,
            send_sem=xs_sem.at[x],
            recv_sem=xr_sem.at[x],
            device_id=who,
            device_id_type=MESH,
        )

    def drain(ref, sem):
        pltpu.make_async_copy(ref, ref, sem).wait()

    def local_twice(src, dst, x):
        pltpu.make_async_copy(src, dst, xr_sem.at[x]).start()
        pltpu.make_async_copy(src, dummy.at[x], xs_sem.at[x]).start()

    def half_peers(visit):
        for db in range(4):
            bb = lax.rem(lax.div(px, 2) + db, 4)

            @pl.loop(0, 8)
            def _(a, bb=bb):
                row = lax.rem(py + a, 8)
                visit(4 * row + bb, row, 2 * bb + par)

    def start_or_keep(src, dst, x, cc, row, col):
        same = jnp.logical_and(cc == c, jnp.logical_and(row == py, col == px))

        @pl.when(jnp.logical_not(same))
        def _():
            remote(src, dst, x, (cc, row, col)).start()

        @pl.when(same)
        def _():
            local_twice(src, dst, x)

    def send_field(x, f, field, fs, fr):
        @pl.loop(0, 8)
        def _(i):
            for j in range(4):
                m = 4 * i + j
                fs[f, m] = field[spot_of(2 * m + par)]

        def visit(m, row, col):
            start_or_keep(fs.at[f, m], fr.at[half, f], x, c, row, col)

        half_peers(visit)

    def send_all(x, f, field):
        @pl.loop(0, 16)
        def _(i):
            for j in range(4):
                r = 4 * i + j
                f3s[f, r] = field[spot_of(r)]

        for db in range(8):
            col = lax.rem(px + db, 8)

            @pl.loop(0, 8)
            def _(a, col=col):
                row = lax.rem(py + a, 8)
                r = 8 * row + col
                start_or_keep(f3s.at[f, r], f3r.at[f, me], x, 1, row, col)

    def first_heat():
        @pl.loop(0, CY)
        def _(y):
            for xb in range(4):
                s = y * 4 + xb
                two = 2 * y + xb // 2
                new = tfl[s] + 0.02 * wet_o[y + 1, pl.ds(8 * xb, 8), :] * asum0[two, xb % 2]
                tfl[s] = new
                b1[2, y + 1, pl.ds(8 * xb, 8), :] = new

    flux0 = [remote(link.at[f, :, 1 - par], f0r.at[:, f], 1 + f, (0, py, px)) for f in range(2)]
    lagged = remote(asum0, asum0, 0, (1, py, px))
    pair2 = remote(own2, a2r, 8, (1, py, px))

    def second_ocean(c_one):
        ocean(b1, b2, True, True, True)
        if c_one:
            send_edges(2, b2, 0, 2)
        send_field(5, 0, rise, f2s, f2r)
        send_field(6, 1, tfl, f2s, f2r)

    def first_tracer():
        tracer(f0r, None, 0, NS)
        light(own1)

        def visit(n, row, col):
            remote(own1.at[n], a1r.at[me], 7, (1, row, col)).start()

        half_peers(visit)

    ld_uv.wait()
    ld_t.wait()
    send_edges(0, b0)

    @pl.when(c == 0)
    def _():
        pltpu.make_async_copy(link, bands0, lsem.at[3]).wait()

        @pl.loop(0, 8)
        def _(i):
            sl = pl.ds(i * 4, 4)
            asum0[sl] = bands0[0, sl] + bands0[1, sl]

        lagged.start()

    @pl.when(c == 1)
    def _():
        for f in range(2):
            flux0[f].start()
        for f in range(2):
            ld_link(f).wait()

    ld_c.wait()
    first_chl()
    light(None)
    take_edges(0, b0)
    ocean(b0, b1, True, True, True)

    @pl.when(c == 0)
    def _():
        first_heat()
        send_edges(1, b1)
        send_field(3, 0, rise, f1s, f1r)
        send_field(4, 1, tfl, f1s, f1r)
        take_edges(1, b1)
        second_ocean(False)
        for f in range(2):
            flux0[f].wait_recv()
        first_tracer()

    @pl.when(c == 1)
    def _():
        send_edges(1, b1, 0, 2)
        send_field(3, 0, rise, f1s, f1r)
        first_tracer()
        lagged.wait_recv()
        first_heat()
        send_edges(4, b1, 2, 3)
        send_field(4, 1, tfl, f1s, f1r)
        take_edges(1, b1, 0, 2)
        take_edges(4, b1, 2, 3)
        second_ocean(True)

    drain(f1r.at[:, 0], xr_sem.at[3])
    drain(f1r.at[:, 1], xr_sem.at[4])
    tracer(f1r, None, 0, NS)
    light(own2)

    @pl.when(c == 0)
    def _():
        pair2.start()

    @pl.when(c == 1)
    def _():
        take_edges(2, b2, 0, 2)
        ocean(b2, None, False, False, True)
        send_all(9, 0, rise)
        drain(a1r, xr_sem.at[7])

        @pl.loop(0, CY)
        def _(y):
            for xb in range(4):
                s = y * 4 + xb
                b2[2, y + 1, pl.ds(8 * xb, 8), :] = tfl[s] + 0.02 * a1r[own_s[me, s]]

        send_edges(3, b2, 2, 3)

    drain(f2r.at[:, 0], xr_sem.at[5])
    drain(f2r.at[:, 1], xr_sem.at[6])
    for j in range(2):
        tracer(f2r, own1, 16 * j, 16 * j + 16)

        @pl.loop(0, 16)
        def _(k):
            n = 16 * j + k
            start_or_keep(
                chl_b.at[n], a3r.at[me], 11, 0, lax.div(n, 4), 2 * lax.rem(n, 4) + par
            )

        if j == 0:

            @pl.when(c == 1)
            def _():
                take_edges(3, b2, 2, 3)
                ocean(b2, None, False, True, False)
                send_all(10, 1, tfl)

    wait_edge_sends(0, b0)
    drain(f1s.at[0], xs_sem.at[3])
    drain(f1s.at[1], xs_sem.at[4])
    drain(f2s.at[0], xs_sem.at[5])
    drain(f2s.at[1], xs_sem.at[6])
    drain(own1, xs_sem.at[7])

    @pl.when(c == 0)
    def _():
        lagged.wait_send()
        pair2.wait_send()
        wait_edge_sends(1, b1)
        drain(a3r, xr_sem.at[11])

        @pl.loop(0, 8)
        def _(i):
            x = jnp.concatenate([a3r[own_s[me, i * 8 + j]] for j in range(8)], axis=0)
            i0, i1, h0, h1 = bands_of(x)
            wet = jnp.concatenate(
                [
                    wet_o[i * 2 + 1 + j // 4, pl.ds(8 * (j % 4), 8), :]
                    for j in range(8)
                ],
                axis=0,
            )
            sl = pl.ds(i * 8, 8)
            out[0, sl] = (wet * i0 * (1.0 - h0 * h0)).reshape(8, 8, K)
            out[1, sl] = (wet * i1 * (1.0 - h1 * h1)).reshape(8, 8, K)

    @pl.when(c == 1)
    def _():
        for f in range(2):
            flux0[f].wait_send()
        wait_edge_sends(1, b1, 0, 2)
        wait_edge_sends(4, b1, 2, 3)
        wait_edge_sends(2, b2, 0, 2)
        wait_edge_sends(3, b2, 2, 3)
        drain(f3s.at[0], xs_sem.at[9])
        drain(f3s.at[1], xs_sem.at[10])
        pair2.wait_recv()
        drain(f3r.at[0], xr_sem.at[9])
        drain(f3r.at[1], xr_sem.at[10])

        @pl.loop(0, NS)
        def _(n):
            mine = 2 * n + par
            other = 2 * n + (1 - par)
            out[0, mine] = f3r[0, mine]
            out[0, other] = f3r[0, other]
            out[1, mine] = f3r[1, mine] + 0.02 * own2[n]
            out[1, other] = f3r[1, other] + 0.02 * a2r[n]

    drain(chl_b, xs_sem.at[11])


def shards(
    current_speeds,
    thermal_anomaly,
    solute_amounts,
    delayed_link_source,
    marine_indicator,
    floor_layer_index,
    holder_rank,
    biota_exchange_matrix,
    photic_absorb_share,
    chroma_loading,
):
    any_spec = pl.BlockSpec(memory_space=pl.ANY)
    vmem = pl.BlockSpec(memory_space=pltpu.VMEM)
    smem = pl.BlockSpec(memory_space=pltpu.SMEM)

    def v(*shape, dtype=F32):
        return pltpu.VMEM(shape, dtype)

    dma = pltpu.SemaphoreType.DMA
    res = pl.pallas_call(
        kernel,
        out_shape=jax.ShapeDtypeStruct((2, NP, SC, K), F32),
        in_specs=[smem] * 3 + [any_spec] * 4 + [vmem] * 4,
        out_specs=vmem,
        scratch_shapes=[
            v(8, 128, dtype=jnp.int32),
            pltpu.SMEM((8, 128), jnp.int32),
            v(128, K),
            v(NS, SC, 128),
            v(NS, SC, K),
            v(18, 40, K),
            v(17, 32, K),
            v(5, 32, K),
            v(128, K),
            v(128, K),
            v(3, 18, 40, K),
            v(3, 18, 40, K),
            v(3, 18, 40, K),
            v(18, 40, K),
            v(18, 40, K),
            v(3, K, K, dtype=BF16),
            v(K, K, dtype=BF16),
            v(NTR, NS, SC, K),
            v(NS, SC, K),
            v(NS, SC, K),
            v(NP, SC, K),
            v(NP, SC, K),
            v(NP, SC, K),
            v(2, NS, 2, SC, K),
            v(NS, 2, SC, K),
            v(NS, 2, SC, K),
            v(2, NS, SC, K),
            v(NS, 2, SC, K),
            v(2, NS, SC, K),
            v(NS, 2, SC, K),
            v(2, NP, SC, K),
            v(2, NP, SC, K),
            v(NS, SC, K),
            v(NS, SC, K),
            v(NP, SC, K),
            v(NS, SC, K),
            v(NP, SC, K),
            v(12, SC, K),
            v(5, 2, 3, CY, K),
            v(5, 2, 3, CY, K),
            dma((7,)),
            dma((5, 4)),
            dma((5, 4)),
            dma((12,)),
            dma((12,)),
        ],
        compiler_params=pltpu.CompilerParams(
            collective_id=0, has_side_effects=True, vmem_limit_bytes=60 * 1024 * 1024
        ),
    )(
        holder_rank,
        photic_absorb_share,
        chroma_loading,
        current_speeds,
        thermal_anomaly,
        solute_amounts.reshape(NTR, NS, 2, SC, K),
        delayed_link_source.reshape(2, NS, 2, SC, K),
        marine_indicator,
        floor_layer_index,
        holder_rank,
        biota_exchange_matrix,
    )
    return res.reshape(1, 2, 1, 512, K)


def solution(mesh):
    placed = (
        P(None, "py", "px", None),
        P("py", "px", None),
        P(None, ("py", "px"), None, None),
        P("comp", None, ("py", "px"), None, None),
        P(),
        P(),
        P(),
        P(),
        P(),
        P(),
    )
    return jax.shard_map(
        shards,
        mesh=mesh,
        in_specs=placed,
        out_specs=P("comp", None, ("py", "px"), None, None),
        check_vma=False,
    )
```

time: 94.6 us -> 77.5 us (0.82)
  the two profiles are of different devices: /device:TPU:25 before, /device:TPU:27 now
where the time goes in v2:
time: 77.5 us; the launch traced here: 77.3 us
  Pallas kernels  75 us (97%)
  local copies, waits for them, and re-layouts  2.26 us (3%)
    pallas_call x1, Pallas kernels, shards(): pl.pallas_call(kernel, out_shape=jax.ShapeDtypeStruct((2, NP, SC, K), F32...  75 us
    unnamed x1, local copies, waits for them, and re-layouts  2.26 us

profile of v2, /device:TPU:27, one launch (start us, length us, event | category | flops | bytes accessed | tf_op | source)
XLA Modules:
  0.0 77.3 jit_solution(17954919033714887942)
XLA Ops:
  0.0 75.0 %shard_map.100 = f32[2,64,8,256]{3,2,1,0:T(8,128)} custom-call(s32[64,64]{1,0:T(8,128)} %owners.1, f32[16]{0:T(128)} %share_s.1, f32[16]{0:T(128)} %load_s.1, f32[2,16,32,256]{3,2,1,0:T(8,128)} %speeds.1, f32[16,32,256]{2,1,0:T(8,128)} %thermal.1, f32[16,32,2,8,256]{4,3,2,1,0:T(8,128)} %bitcast.5, f32[2,32,2,8,256]{4,3,2,1,0:T(8,128)} %bitcast.7, ...), custom_call_target="tpu_custom_call" | custom-call | tf_op jit(solution)/shard_map/pallas_call | solution.py:715
  75.0 2.3 %copy.13 = f32[1,2,1,512,256]{4,3,2,1,0:T(8,128)} copy(f32[1,2,1,512,256]{4,3,2,1,0:T(8,128)} %bitcast.6) | data formatting | bytes 2097152

commit v3 on v2

--- a/solution.py
+++ b/solution.py
@@ -126,102 +126,26 @@
     ld_c.start()
 
     barrier = pltpu.get_barrier_semaphore()
-    for dc in range(2):
+    def greet(dc, a, db):
+        pl.semaphore_signal(
+            barrier,
+            inc=1,
+            device_id=(lax.rem(c + dc, 2), lax.rem(py + a, 8), lax.rem(px + db, 8)),
+            device_id_type=MESH,
+        )
+
+    @pl.loop(1, 8)
+    def _(a):
         for db in range(8):
-
-            @pl.loop(1 if dc == 0 and db == 0 else 0, 8)
-            def _(a, dc=dc, db=db):
-                pl.semaphore_signal(
-                    barrier,
-                    inc=1,
-                    device_id=(lax.rem(c + dc, 2), lax.rem(py + a, 8), lax.rem(px + db, 8)),
-                    device_id_type=MESH,
-                )
-
-    step64 = lax.broadcasted_iota(jnp.int32, (NP, NP), 1).astype(F32)
-    row64 = lax.broadcasted_iota(jnp.int32, (NP, NP), 0)
-    held = jnp.where(owners[...] == me, 1.0, 0.0).astype(F32)
-    placed = jnp.where(
-        jnp.broadcast_to(owners[pl.ds(me, 1), :], (NP, NP)) == row64, 1.0, 0.0
-    ).astype(F32)
-    nt = (((1,), (1,)), ((), ()))
-    steps8 = step64[0:8]
-    for j, spots in enumerate((placed, held)):
-        found = lax.dot_general(steps8, spots, nt, preferred_element_type=F32)
-        inv_v[0:8, 64 * j : 64 * j + 64] = jnp.minimum(found, NP - 1.0).astype(jnp.int32)
-    to_smem = pltpu.make_async_copy(inv_v, inv_s, lsem.at[6])
-    to_smem.start()
-
-    rows = lax.broadcasted_iota(jnp.int32, (K, K), 0)
-    cols = lax.broadcasted_iota(jnp.int32, (K, K), 1)
-    tabs[0] = jnp.where(rows < cols, 1.0, jnp.where(rows == cols, 0.5, 0.0)).astype(BF16)
-    tabs[1] = jnp.where(rows >= cols, 1.0, 0.0).astype(BF16)
-    tabs[2] = jnp.where(rows < cols, 1.0, 0.0).astype(BF16)
-    r16 = lax.broadcasted_iota(jnp.int32, (128, 16), 0)
-    c16 = lax.broadcasted_iota(jnp.int32, (128, 16), 1)
-    spread = jnp.where(lax.shift_right_logical(r16, 3) == c16, 1.0, 0.0).astype(F32)
-    r16t = lax.broadcasted_iota(jnp.int32, (16, 128), 0)
-    c16t = lax.broadcasted_iota(jnp.int32, (16, 128), 1)
-    spread_t = jnp.where(lax.shift_right_logical(c16t, 3) == r16t, 1.0, 0.0).astype(F32)
-    wide = jnp.dot(
-        jnp.dot(spread, mix[...], precision=lax.Precision.HIGHEST, preferred_element_type=F32),
-        spread_t,
-        precision=lax.Precision.HIGHEST,
-        preferred_element_type=F32,
-    )
-    r128 = lax.broadcasted_iota(jnp.int32, (128, 128), 0)
-    c128 = lax.broadcasted_iota(jnp.int32, (128, 128), 1)
-    same = lax.bitwise_and(r128, 7) == lax.bitwise_and(c128, 7)
-    wide = jnp.where(same, wide, 0.0)
-    whi, wlo = split(wide)
-    wmix[0:128, 0:128] = whi
-    wmix[0:128, 128:256] = whi
-    wmix[128:256, 0:128] = wlo
-    wmix[128:256, 128:256] = jnp.zeros((128, 128), BF16)
-
-    ones = jnp.ones((K, 128), BF16)
-    depth[...] = (marine[...] * floor[...]).astype(F32)
-    lev40 = lax.broadcasted_iota(jnp.int32, (40, 128), 1).astype(F32)
-    spot = lax.broadcasted_iota(jnp.int32, (40, K), 0)
-    spot = jnp.where(spot < 36, spot, spot - 40)
-    column = lax.broadcasted_iota(jnp.int32, (40, K), 1)
-    chosen = lax.bitwise_and(spot + (px * CX + K), K - 1) == column
-
-    @pl.loop(0, 18)
-    def _(y):
-        gy = py * CY + y - 1
-        inside = jnp.logical_and(gy >= 0, gy < 128)
-        line = depth[pl.ds(jnp.clip(gy, 0, 127), 1), :]
-        line = line * jnp.where(inside, 1.0, 0.0).astype(F32)
-        d = dot(jnp.where(chosen, line, 0.0).astype(BF16), ones)
-        w = jnp.concatenate(
-            [
-                jnp.where(lev40 < d, 1.0, 0.0).astype(F32),
-                jnp.where(lev40 + 128.0 < d, 1.0, 0.0).astype(F32),
-            ],
-            axis=1,
-        )
-        wet_o[y] = w
-        face_x[y] = w * pltpu.roll(w, 39, 0)
-
-    @pl.loop(0, 17)
-    def _(y):
-        face_y[y] = wet_o[y, 0:32, :] * wet_o[y + 1, 0:32, :]
-
-    to_smem.wait()
-    ahead = lax.broadcasted_iota(jnp.int32, (8, K), 1) - lax.broadcasted_iota(
-        jnp.int32, (8, K), 0
-    )
-
-    @pl.loop(0, NS)
-    def _(n):
-        q = 2 * n + par
-        s = spot_of(64 + q)
-        line = depth[lax.div(q, 8) * CY + lax.shift_right_logical(s, 2)]
-        x0 = lax.rem(q, 8) * CX + lax.bitwise_and(s, 3) * 8
-        pick[n] = jnp.where(ahead == x0, jnp.broadcast_to(line[None, :], (8, K)), 0.0)
-
-    depth_t[...] = dot(pick[...].reshape(NS * 8, K).astype(BF16), ones).reshape(NS, 8, 128)
+            greet(0, a, db)
+
+    for db in range(1, 8):
+        greet(0, 0, db)
+
+    @pl.loop(0, 8)
+    def _(a):
+        for db in range(8):
+            greet(1, a, db)
 
     north = (c, lax.rem(py + 1, 8), px)
     south = (c, lax.rem(py + 7, 8), px)
@@ -379,12 +303,13 @@
             chl_b[n] = total
 
     def mingle(n, dest):
-        hi_x, lo_x = split(conc[:, n].reshape(128, K))
-        y = dot(wmix[...], jnp.concatenate([hi_x, lo_x], axis=0))
-        dest[...] = y[0:128] + y[128:256]
+        for j in range(2):
+            hi_x, lo_x = split(conc[:, n + j].reshape(128, K))
+            y = dot(wmix[...], jnp.concatenate([hi_x, lo_x], axis=0))
+            dest[j] = y[0:128] + y[128:256]
 
     def tracer(flux, extra, lo, hi):
-        def advance(n, mixed):
+        def advance(n, mixed, j):
             up = flux[n, 0]
             heat = flux[n, 1]
             if extra is not None:
@@ -403,7 +328,7 @@
                 ci = conc[i, n]
                 new = (
                     stay * ci
-                    + warm * mixed[8 * i : 8 * i + 8]
+                    + warm * mixed[j, 8 * i : 8 * i + 8]
                     + upper * pltpu.roll(ci, K - 1, 1)
                     - lower * pltpu.roll(ci, 1, 1)
                     + share_s[i] * grow
@@ -415,13 +340,15 @@
 
         mingle(lo, mixed_a)
 
-        @pl.loop(0, (hi - lo) // 2)
+        @pl.loop(0, (hi - lo) // 4)
         def _(k):
-            n = lo + 2 * k
-            mingle(n + 1, mixed_b)
-            advance(n, mixed_a)
-            mingle(jnp.minimum(n + 2, hi - 1), mixed_a)
-            advance(n + 1, mixed_b)
+            n = lo + 4 * k
+            mingle(n + 2, mixed_b)
+            advance(n, mixed_a, 0)
+            advance(n + 1, mixed_a, 1)
+            mingle(jnp.minimum(n + 4, hi - 2), mixed_a)
+            advance(n + 2, mixed_b, 0)
+            advance(n + 3, mixed_b, 1)
 
     lev_f = lax.broadcasted_iota(jnp.int32, (64, K), 1).astype(F32)
 
@@ -459,17 +386,21 @@
         pltpu.make_async_copy(ref, ref, sem).wait()
 
     def local_twice(src, dst, x):
+        spare = dummy.at[x] if len(src.shape) == 3 else dummy.at[x, 0]
         pltpu.make_async_copy(src, dst, xr_sem.at[x]).start()
-        pltpu.make_async_copy(src, dummy.at[x], xs_sem.at[x]).start()
+        pltpu.make_async_copy(src, spare, xs_sem.at[x]).start()
+
+    strip_cols = [lax.rem(lax.div(px, 2) + db, 4) for db in range(4)]
 
     def half_peers(visit):
-        for db in range(4):
-            bb = lax.rem(lax.div(px, 2) + db, 4)
-
-            @pl.loop(0, 8)
-            def _(a, bb=bb):
-                row = lax.rem(py + a, 8)
-                visit(4 * row + bb, row, 2 * bb + par)
+        @pl.loop(1, 8)
+        def _(a):
+            row = lax.rem(py + a, 8)
+            for bb in strip_cols:
+                visit(4 * row + bb, row, 2 * bb + par, False)
+
+        for i, bb in enumerate(strip_cols):
+            visit(4 * py + bb, py, 2 * bb + par, i == 0)
 
     def start_or_keep(src, dst, x, cc, row, col):
         same = jnp.logical_and(cc == c, jnp.logical_and(row == py, col == px))
@@ -482,43 +413,97 @@
         def _():
             local_twice(src, dst, x)
 
-    def send_field(x, f, field, fs, fr):
+    def send_field(x, fields, fs, fr, near=False):
         @pl.loop(0, 8)
         def _(i):
             for j in range(4):
                 m = 4 * i + j
-                fs[f, m] = field[spot_of(2 * m + par)]
-
-        def visit(m, row, col):
-            start_or_keep(fs.at[f, m], fr.at[half, f], x, c, row, col)
-
-        half_peers(visit)
-
-    def send_all(x, f, field):
+                s = spot_of(2 * m + par)
+                for f, field in fields:
+                    fs[m, f] = field[s]
+
+        def visit(m, row, col, maybe):
+            if len(fields) == 2:
+                src, dst = fs.at[m], fr.at[half]
+            else:
+                src, dst = fs.at[m, fields[0][0]], fr.at[half, fields[0][0]]
+            if maybe:
+                start_or_keep(src, dst, x, c, row, col)
+            else:
+                remote(src, dst, x, (c, row, col)).start()
+
+        if near:
+
+            @pl.loop(0, 4)
+            def _(a):
+                row = 4 * lax.div(py, 4) + lax.rem(lax.rem(py, 4) + a, 4)
+                for bb in strip_cols:
+                    visit(4 * row + bb, row, 2 * bb + par, False)
+
+        else:
+            half_peers(visit)
+
+    def send_far():
+        far = 4 - 4 * lax.div(py, 4)
+
+        @pl.loop(0, 4)
+        def _(i):
+            for j in range(4):
+                s = spot_of(2 * (4 * (far + i) + j) + 1 - par)
+                f2s[NS + 4 * i + j, 0] = rise[s]
+                f2s[NS + 4 * i + j, 1] = tfl[s]
+
+        @pl.loop(0, 4)
+        def _(a):
+            i = lax.rem(lax.rem(py, 4) + a, 4)
+            for bb in strip_cols:
+                who = (1, far + i, 2 * bb + 1 - par)
+                remote(f2s.at[NS + 4 * i + bb], f2r.at[half], 5, who).start()
+
+    def send_all(x, f, field, cross):
         @pl.loop(0, 16)
         def _(i):
             for j in range(4):
                 r = 4 * i + j
                 f3s[f, r] = field[spot_of(r)]
 
-        for db in range(8):
-            col = lax.rem(px + db, 8)
-
-            @pl.loop(0, 8)
-            def _(a, col=col):
-                row = lax.rem(py + a, 8)
-                r = 8 * row + col
-                start_or_keep(f3s.at[f, r], f3r.at[f, me], x, 1, row, col)
+        cols8 = [lax.rem(px + db, 8) for db in range(8)]
+        near = 4 * lax.div(py, 4)
+        far = 4 - near
+        place = lax.rem(py, 4)
+
+        def to_row(row, cols):
+            for col in cols:
+                remote(f3s.at[f, 8 * row + col], f3r.at[f, me], x, (1, row, col)).start()
+
+        if cross:
+
+            @pl.loop(0, 4)
+            def _(a):
+                to_row(far + lax.rem(place + a, 4), cols8)
+
+        else:
+
+            @pl.loop(1, 4)
+            def _(a):
+                to_row(near + lax.rem(place + a, 4), cols8)
+
+            to_row(py, cols8[1:])
+            local_twice(f3s.at[f, me], f3r.at[f, me], x)
+            if f == 1:
+
+                @pl.loop(0, 4)
+                def _(a):
+                    to_row(far + lax.rem(place + a, 4), cols8)
 
     def first_heat():
         @pl.loop(0, CY)
         def _(y):
-            for xb in range(4):
-                s = y * 4 + xb
-                two = 2 * y + xb // 2
-                new = tfl[s] + 0.02 * wet_o[y + 1, pl.ds(8 * xb, 8), :] * asum0[two, xb % 2]
-                tfl[s] = new
-                b1[2, y + 1, pl.ds(8 * xb, 8), :] = new
+            s4 = pl.ds(y * 4, 4)
+            gain = wet_o[y + 1, 0:32, :] * asum0[pl.ds(2 * y, 2)].reshape(32, K)
+            new = tfl[s4].reshape(32, K) + 0.02 * gain
+            tfl[s4] = new.reshape(4, 8, K)
+            b1[2, y + 1, 0:32, :] = new
 
     flux0 = [remote(link.at[f, :, 1 - par], f0r.at[:, f], 1 + f, (0, py, px)) for f in range(2)]
     lagged = remote(asum0, asum0, 0, (1, py, px))
@@ -526,16 +511,18 @@
 
     def second_ocean(c_one):
         ocean(b1, b2, True, True, True)
+        send_edges(2, b2, 0, 2)
         if c_one:
-            send_edges(2, b2, 0, 2)
-        send_field(5, 0, rise, f2s, f2r)
-        send_field(6, 1, tfl, f2s, f2r)
+            send_field(5, [(0, rise), (1, tfl)], f2s, f2r, True)
+        else:
+            send_field(5, [(0, rise), (1, tfl)], f2s, f2r)
+            send_far()
 
     def first_tracer():
         tracer(f0r, None, 0, NS)
         light(own1)
 
-        def visit(n, row, col):
+        def visit(n, row, col, maybe):
             remote(own1.at[n], a1r.at[me], 7, (1, row, col)).start()
 
         half_peers(visit)
@@ -561,6 +548,92 @@
             flux0[f].start()
         for f in range(2):
             ld_link(f).wait()
+
+    step64 = lax.broadcasted_iota(jnp.int32, (NP, NP), 1).astype(F32)
+    row64 = lax.broadcasted_iota(jnp.int32, (NP, NP), 0)
+    held = jnp.where(owners[...] == me, 1.0, 0.0).astype(F32)
+    placed = jnp.where(
+        jnp.broadcast_to(owners[pl.ds(me, 1), :], (NP, NP)) == row64, 1.0, 0.0
+    ).astype(F32)
+    nt = (((1,), (1,)), ((), ()))
+    steps8 = step64[0:8]
+    for j, spots in enumerate((placed, held)):
+        found = lax.dot_general(steps8, spots, nt, preferred_element_type=F32)
+        inv_v[0:8, 64 * j : 64 * j + 64] = jnp.minimum(found, NP - 1.0).astype(jnp.int32)
+    to_smem = pltpu.make_async_copy(inv_v, inv_s, lsem.at[6])
+    to_smem.start()
+
+    rows = lax.broadcasted_iota(jnp.int32, (K, K), 0)
+    cols = lax.broadcasted_iota(jnp.int32, (K, K), 1)
+    tabs[0] = jnp.where(rows < cols, 1.0, jnp.where(rows == cols, 0.5, 0.0)).astype(BF16)
+    tabs[1] = jnp.where(rows >= cols, 1.0, 0.0).astype(BF16)
+    tabs[2] = jnp.where(rows < cols, 1.0, 0.0).astype(BF16)
+    r16 = lax.broadcasted_iota(jnp.int32, (128, 16), 0)
+    c16 = lax.broadcasted_iota(jnp.int32, (128, 16), 1)
+    spread = jnp.where(lax.shift_right_logical(r16, 3) == c16, 1.0, 0.0).astype(F32)
+    r16t = lax.broadcasted_iota(jnp.int32, (16, 128), 0)
+    c16t = lax.broadcasted_iota(jnp.int32, (16, 128), 1)
+    spread_t = jnp.where(lax.shift_right_logical(c16t, 3) == r16t, 1.0, 0.0).astype(F32)
+    wide = jnp.dot(
+        jnp.dot(spread, mix[...], precision=lax.Precision.HIGHEST, preferred_element_type=F32),
+        spread_t,
+        precision=lax.Precision.HIGHEST,
+        preferred_element_type=F32,
+    )
+    r128 = lax.broadcasted_iota(jnp.int32, (128, 128), 0)
+    c128 = lax.broadcasted_iota(jnp.int32, (128, 128), 1)
+    same = lax.bitwise_and(r128, 7) == lax.bitwise_and(c128, 7)
+    wide = jnp.where(same, wide, 0.0)
+    whi, wlo = split(wide)
+    wmix[0:128, 0:128] = whi
+    wmix[0:128, 128:256] = whi
+    wmix[128:256, 0:128] = wlo
+    wmix[128:256, 128:256] = jnp.zeros((128, 128), BF16)
+
+    ones = jnp.ones((K, 128), BF16)
+    depth[...] = (marine[...] * floor[...]).astype(F32)
+    lev40 = lax.broadcasted_iota(jnp.int32, (40, 128), 1).astype(F32)
+    spot = lax.broadcasted_iota(jnp.int32, (40, K), 0)
+    spot = jnp.where(spot < 36, spot, spot - 40)
+    column = lax.broadcasted_iota(jnp.int32, (40, K), 1)
+    chosen = lax.bitwise_and(spot + (px * CX + K), K - 1) == column
+
+    @pl.loop(0, 18)
+    def _(y):
+        gy = py * CY + y - 1
+        inside = jnp.logical_and(gy >= 0, gy < 128)
+        line = depth[pl.ds(jnp.clip(gy, 0, 127), 1), :]
+        line = line * jnp.where(inside, 1.0, 0.0).astype(F32)
+        d = dot(jnp.where(chosen, line, 0.0).astype(BF16), ones)
+        w = jnp.concatenate(
+            [
+                jnp.where(lev40 < d, 1.0, 0.0).astype(F32),
+                jnp.where(lev40 + 128.0 < d, 1.0, 0.0).astype(F32),
+            ],
+            axis=1,
+        )
+        wet_o[y] = w
+        face_x[y] = w * pltpu.roll(w, 39, 0)
+
+    @pl.loop(0, 17)
+    def _(y):
+        face_y[y] = wet_o[y, 0:32, :] * wet_o[y + 1, 0:32, :]
+
+    to_smem.wait()
+    ahead = lax.broadcasted_iota(jnp.int32, (8, K), 1) - lax.broadcasted_iota(
+        jnp.int32, (8, K), 0
+    )
+
+    @pl.loop(0, 8)
+    def _(i):
+        for j in range(4):
+            n = 4 * i + j
+            s = spot_of(64 + 2 * n + par)
+            line = depth[i * CY + lax.shift_right_logical(s, 2)]
+            x0 = (2 * j + par) * CX + lax.bitwise_and(s, 3) * 8
+            pick[n] = jnp.where(ahead == x0, jnp.broadcast_to(line[None, :], (8, K)), 0.0)
+
+    depth_t[...] = dot(pick[...].reshape(NS * 8, K).astype(BF16), ones).reshape(NS, 8, 128)
 
     ld_c.wait()
     first_chl()
@@ -572,62 +645,83 @@
     def _():
         first_heat()
         send_edges(1, b1)
-        send_field(3, 0, rise, f1s, f1r)
-        send_field(4, 1, tfl, f1s, f1r)
-        take_edges(1, b1)
-        second_ocean(False)
+        send_field(3, [(0, rise), (1, tfl)], f1s, f1r)
         for f in range(2):
             flux0[f].wait_recv()
         first_tracer()
+        take_edges(1, b1)
+        second_ocean(False)
 
     @pl.when(c == 1)
     def _():
         send_edges(1, b1, 0, 2)
-        send_field(3, 0, rise, f1s, f1r)
+        send_field(3, [(0, rise)], f1s, f1r)
         first_tracer()
         lagged.wait_recv()
         first_heat()
         send_edges(4, b1, 2, 3)
-        send_field(4, 1, tfl, f1s, f1r)
+        send_field(4, [(1, tfl)], f1s, f1r)
         take_edges(1, b1, 0, 2)
         take_edges(4, b1, 2, 3)
         second_ocean(True)
 
-    drain(f1r.at[:, 0], xr_sem.at[3])
-    drain(f1r.at[:, 1], xr_sem.at[4])
+    @pl.when(c == 0)
+    def _():
+        drain(f1r, xr_sem.at[3])
+
+    @pl.when(c == 1)
+    def _():
+        drain(f1r.at[:, 0], xr_sem.at[3])
+        drain(f1r.at[:, 1], xr_sem.at[4])
+
     tracer(f1r, None, 0, NS)
     light(own2)
 
     @pl.when(c == 0)
     def _():
         pair2.start()
-
-    @pl.when(c == 1)
-    def _():
         take_edges(2, b2, 0, 2)
         ocean(b2, None, False, False, True)
-        send_all(9, 0, rise)
+        send_all(9, 0, rise, True)
+
+    @pl.when(c == 1)
+    def _():
         drain(a1r, xr_sem.at[7])
 
-        @pl.loop(0, CY)
-        def _(y):
-            for xb in range(4):
-                s = y * 4 + xb
-                b2[2, y + 1, pl.ds(8 * xb, 8), :] = tfl[s] + 0.02 * a1r[own_s[me, s]]
+        @pl.loop(0, 8)
+        def _(i):
+            for j in range(8):
+                y = 2 * i + j // 4
+                s = 8 * i + j
+                b2[2, y + 1, pl.ds(8 * (j % 4), 8), :] = tfl[s] + 0.02 * a1r[own_s[me, s]]
 
         send_edges(3, b2, 2, 3)
-
-    drain(f2r.at[:, 0], xr_sem.at[5])
-    drain(f2r.at[:, 1], xr_sem.at[6])
+        take_edges(2, b2, 0, 2)
+        ocean(b2, None, False, False, True)
+        send_all(9, 0, rise, False)
+
+    drain(f2r, xr_sem.at[5])
     for j in range(2):
         tracer(f2r, own1, 16 * j, 16 * j + 16)
 
-        @pl.loop(0, 16)
-        def _(k):
-            n = 16 * j + k
-            start_or_keep(
-                chl_b.at[n], a3r.at[me], 11, 0, lax.div(n, 4), 2 * lax.rem(n, 4) + par
-            )
+        @pl.when(c == 0)
+        def _(j=j):
+            @pl.loop(0, 16)
+            def _(k):
+                n = 16 * j + k
+                start_or_keep(
+                    chl_b.at[n], a3r.at[me], 11, 0, lax.div(n, 4), 2 * lax.rem(n, 4) + par
+                )
+
+        @pl.when(c == 1)
+        def _(j=j):
+            @pl.loop(0, 4)
+            def _(a):
+                row = 4 * j + lax.rem(py + a, 4)
+                for bb in strip_cols:
+                    remote(
+                        chl_b.at[4 * row + bb], a3r.at[me], 11, (0, row, 2 * bb + par)
+                    ).start()
 
         if j == 0:
 
@@ -635,13 +729,9 @@
             def _():
                 take_edges(3, b2, 2, 3)
                 ocean(b2, None, False, True, False)
-                send_all(10, 1, tfl)
+                send_all(10, 1, tfl, False)
 
     wait_edge_sends(0, b0)
-    drain(f1s.at[0], xs_sem.at[3])
-    drain(f1s.at[1], xs_sem.at[4])
-    drain(f2s.at[0], xs_sem.at[5])
-    drain(f2s.at[1], xs_sem.at[6])
     drain(own1, xs_sem.at[7])
 
     @pl.when(c == 0)
@@ -649,6 +739,10 @@
         lagged.wait_send()
         pair2.wait_send()
         wait_edge_sends(1, b1)
+        wait_edge_sends(2, b2, 0, 2)
+        drain(f3s.at[0, 0:32], xs_sem.at[9])
+        drain(f1s, xs_sem.at[3])
+        drain(f2s, xs_sem.at[5])
         drain(a3r, xr_sem.at[11])
 
         @pl.loop(0, 8)
@@ -670,11 +764,14 @@
     def _():
         for f in range(2):
             flux0[f].wait_send()
+        drain(f1s.at[:, 0], xs_sem.at[3])
+        drain(f2s.at[0:16], xs_sem.at[5])
+        drain(f1s.at[:, 1], xs_sem.at[4])
         wait_edge_sends(1, b1, 0, 2)
         wait_edge_sends(4, b1, 2, 3)
         wait_edge_sends(2, b2, 0, 2)
         wait_edge_sends(3, b2, 2, 3)
-        drain(f3s.at[0], xs_sem.at[9])
+        drain(f3s.at[0, 0:32], xs_sem.at[9])
         drain(f3s.at[1], xs_sem.at[10])
         pair2.wait_recv()
         drain(f3r.at[0], xr_sem.at[9])
@@ -726,8 +823,8 @@
             v(18, 40, K),
             v(17, 32, K),
             v(5, 32, K),
-            v(128, K),
-            v(128, K),
+            v(2, 128, K),
+            v(2, 128, K),
             v(3, 18, 40, K),
             v(3, 18, 40, K),
             v(3, 18, 40, K),
@@ -744,9 +841,9 @@
             v(2, NS, 2, SC, K),
             v(NS, 2, SC, K),
             v(NS, 2, SC, K),
-            v(2, NS, SC, K),
             v(NS, 2, SC, K),
-            v(2, NS, SC, K),
+            v(NS, 2, SC, K),
+            v(48, 2, SC, K),
             v(NS, 2, SC, K),
             v(2, NP, SC, K),
             v(2, NP, SC, K),
@@ -755,7 +852,7 @@
             v(NP, SC, K),
             v(NS, SC, K),
             v(NP, SC, K),
-            v(12, SC, K),
+            v(12, 2, SC, K),
             v(5, 2, 3, CY, K),
             v(5, 2, 3, CY, K),
             dma((7,)),

time: 77.5 us -> 69.8 us (0.901)
  the two profiles are of different devices: /device:TPU:27 before, /device:TPU:2 now
where the time goes in v3:
time: 69.8 us; the launch traced here: 69.6 us
  Pallas kernels  67.4 us (97%)
  local copies, waits for them, and re-layouts  2.26 us (3%)
    pallas_call x1, Pallas kernels, shards(): pl.pallas_call(kernel, out_shape=jax.ShapeDtypeStruct((2, NP, SC, K), F32...  67.4 us
    unnamed x1, local copies, waits for them, and re-layouts  2.26 us

profile of v3, /device:TPU:2, one launch (start us, length us, event | category | flops | bytes accessed | tf_op | source)
XLA Modules:
  0.0 69.6 jit_solution(8438268068395445580)
XLA Ops:
  0.0 67.4 %shard_map.100 = f32[2,64,8,256]{3,2,1,0:T(8,128)} custom-call(s32[64,64]{1,0:T(8,128)} %owners.1, f32[16]{0:T(128)} %share_s.1, f32[16]{0:T(128)} %load_s.1, f32[2,16,32,256]{3,2,1,0:T(8,128)} %speeds.1, f32[16,32,256]{2,1,0:T(8,128)} %thermal.1, f32[16,32,2,8,256]{4,3,2,1,0:T(8,128)} %bitcast.5, f32[2,32,2,8,256]{4,3,2,1,0:T(8,128)} %bitcast.7, ...), custom_call_target="tpu_custom_call" | custom-call | tf_op jit(solution)/shard_map/pallas_call | solution.py:812
  67.4 2.3 %copy.13 = f32[1,2,1,512,256]{4,3,2,1,0:T(8,128)} copy(f32[1,2,1,512,256]{4,3,2,1,0:T(8,128)} %bitcast.6) | data formatting | bytes 2097152

commit v4 on v3

--- a/solution.py
+++ b/solution.py
@@ -701,23 +701,22 @@
         send_all(9, 0, rise, False)
 
     drain(f2r, xr_sem.at[5])
-    for j in range(2):
-        tracer(f2r, own1, 16 * j, 16 * j + 16)
+    for j, (top, end) in enumerate(((0, 2), (2, 5), (5, 8))):
+        tracer(f2r, own1, 4 * top, 4 * end)
 
         @pl.when(c == 0)
-        def _(j=j):
-            @pl.loop(0, 16)
-            def _(k):
-                n = 16 * j + k
+        def _(top=top, end=end):
+            @pl.loop(4 * top, 4 * end)
+            def _(n):
                 start_or_keep(
                     chl_b.at[n], a3r.at[me], 11, 0, lax.div(n, 4), 2 * lax.rem(n, 4) + par
                 )
 
         @pl.when(c == 1)
-        def _(j=j):
-            @pl.loop(0, 4)
+        def _(top=top, end=end):
+            @pl.loop(0, end - top)
             def _(a):
-                row = 4 * j + lax.rem(py + a, 4)
+                row = top + lax.rem(py + a, end - top)
                 for bb in strip_cols:
                     remote(
                         chl_b.at[4 * row + bb], a3r.at[me], 11, (0, row, 2 * bb + par)

time: 69.8 us -> 69 us (0.989)
  Pallas kernels: 67.4 us -> 66.5 us
    pallas_call x1, Pallas kernels: 67.4 us -> 66.5 us  [shards(): pl.pallas_call(kernel, out_shape=jax.ShapeDtypeStruct((2, NP, SC, K), F32...]
where the time goes in v4:
time: 69 us; the launch traced here: 68.8 us
  Pallas kernels  66.5 us (96%)
  local copies, waits for them, and re-layouts  2.26 us (3%)
    pallas_call x1, Pallas kernels, shards(): pl.pallas_call(kernel, out_shape=jax.ShapeDtypeStruct((2, NP, SC, K), F32...  66.5 us
    unnamed x1, local copies, waits for them, and re-layouts  2.26 us

profile of v4, /device:TPU:2, one launch (start us, length us, event | category | flops | bytes accessed | tf_op | source)
XLA Modules:
  0.0 68.8 jit_solution(3102763034985296963)
XLA Ops:
  0.0 66.5 %shard_map.100 = f32[2,64,8,256]{3,2,1,0:T(8,128)} custom-call(s32[64,64]{1,0:T(8,128)} %owners.1, f32[16]{0:T(128)} %share_s.1, f32[16]{0:T(128)} %load_s.1, f32[2,16,32,256]{3,2,1,0:T(8,128)} %speeds.1, f32[16,32,256]{2,1,0:T(8,128)} %thermal.1, f32[16,32,2,8,256]{4,3,2,1,0:T(8,128)} %bitcast.5, f32[2,32,2,8,256]{4,3,2,1,0:T(8,128)} %bitcast.7, ...), custom_call_target="tpu_custom_call" | custom-call | tf_op jit(solution)/shard_map/pallas_call | solution.py:811
  66.5 2.3 %copy.13 = f32[1,2,1,512,256]{4,3,2,1,0:T(8,128)} copy(f32[1,2,1,512,256]{4,3,2,1,0:T(8,128)} %bitcast.6) | data formatting | bytes 2097152
